TPU v7x, 512 devices: a whole 4x8x8 slice. The times are simulated.
512 devices in a mesh: rows: 64 (over x, y, core), feat: 8 (over z).
Axes of the slice: x: 4, y: 8, z: 8, core: 2. Of those that a mesh axis runs over, the one named last changes fastest.
Arguments:
- scores: float32 [131072], P(('rows', 'feat')), may hold values from -6 to 6
- weights: float32 [131072], P(('rows', 'feat')), may hold values from 0.25 to 4
- labels: int32 [131072], P(('rows', 'feat')), may hold values from 0 to 4
- owner_row: int32 [131072], P(('rows', 'feat')), may hold values from 0 to 63, as said below
- owner_slot: int32 [131072], P(('rows', 'feat')), may hold values from 0 to 255, as said below
- query_len: int32 [512, 4], P(('rows', 'feat')), may hold values from 1 to 128, 256 in all within a row
- bin_index: int32 [512, 131072], P('feat', 'rows'), may hold values from 0 to 255
- parent: int32 [131072], P('rows'), may hold values from 0 to 15, as said below
- split_feat: int32 [16], replicated, may hold values from 0 to 511
- split_thr: int32 [16], replicated, may hold values from 0 to 254
Outputs:
- histogram: float32 [64, 512, 256], P('rows', 'feat')
- new_node: int32 [131072], P(('rows', 'feat'))
Inputs may be any that keep to these rules, and one draw needn't show every extreme that they name: `owner_row`: documents move only along rows: an owner keeps the sender's feat index. One device holds at most 8 documents of one owner, exactly 8 for some device and owner in every draw, and every owner owns exactly 256 documents. The documents of one owner carry distinct owner_slot values, each of 0 to 255 once. The lengths in one row of query_len sum to 256. Among the documents of one index of rows, each parent node holds at most 160, and some parent holds exactly 160 in every index of rows.
All inputs are finite; a program needn't handle non-finite values.
Results may differ from a plain program's by a relative error of at most 0.0028.
Values may be sent and summed in bfloat16 or wider, within the bound.
No kernel may reach another device: no remote copies, remote signals or barrier semaphores. Data moves between devices by JAX's collectives and lax.ppermute only.
A program may use at most 64 MiB of HBM per device.

v0:
```python
import math

import jax
import jax.numpy as jnp
from jax import lax
from jax.sharding import PartitionSpec as P

BINS = 256
NODES = 32
QMAX = 128
PARENTS = 16


sigma_scale = 1.0


def query_lambdas(doc_score, weight, doc_label, usable):
    usable_f = usable.astype(jnp.float32)
    doc_gain = (jnp.exp2(doc_label.astype(jnp.float32)) - 1.0) * usable_f
    places = jnp.arange(doc_score.shape[1], dtype=jnp.int32)
    ranked_above = (doc_score[:, None, :] > doc_score[:, :, None]) | (
        doc_score[:, None, :] == doc_score[:, :, None]
    ) & (places[None, None, :] < places[None, :, None])
    doc_rank = 1.0 + jnp.sum(ranked_above.astype(jnp.float32) * usable_f[:, None, :], axis=2)
    discount = 1.0 / jnp.log2(1.0 + doc_rank)
    levels = jnp.arange(1, 5, dtype=jnp.int32)
    counts = jnp.sum(
        ((doc_label[:, :, None] >= levels[None, None, :]) & usable[:, :, None]).astype(jnp.int32),
        axis=1,
    )
    ideal_label = jnp.sum((places[None, :, None] < counts[:, None, :]).astype(jnp.int32), axis=2)
    ideal_gain = jnp.exp2(ideal_label.astype(jnp.float32)) - 1.0
    ideal_dcg = jnp.sum(ideal_gain / jnp.log2(places.astype(jnp.float32) + 2.0)[None, :], axis=1)
    inv_ideal = 1.0 / jnp.maximum(ideal_dcg, 1.0)
    swap_gain = jnp.abs(doc_gain[:, :, None] - doc_gain[:, None, :]) * jnp.abs(
        discount[:, :, None] - discount[:, None, :]
    )
    swap_gain = swap_gain * (weight[:, :, None] * weight[:, None, :]) * inv_ideal[:, None, None]
    better = (
        (doc_label[:, :, None] > doc_label[:, None, :]) & usable[:, :, None] & usable[:, None, :]
    ).astype(jnp.float32)
    misorder = jax.nn.sigmoid(-sigma_scale * (doc_score[:, :, None] - doc_score[:, None, :]))
    pushed = better * misorder * swap_gain
    gradient = sigma_scale * (jnp.sum(pushed, axis=1) - jnp.sum(pushed, axis=2))
    curvature = (better + jnp.swapaxes(better, 1, 2)) * misorder * (1.0 - misorder) * swap_gain
    hessian = sigma_scale * sigma_scale * jnp.sum(curvature, axis=2)
    return (gradient, hessian)


def owner_lambdas(doc_score, weight, doc_label, lengths):
    doc_count = doc_score.shape[0]
    starts = jnp.cumsum(lengths) - lengths
    places = jnp.arange(QMAX, dtype=jnp.int32)
    flat_index = starts[:, None] + places[None, :]
    usable = places[None, :] < lengths[:, None]
    clipped = jnp.clip(flat_index, 0, doc_count - 1)
    gradient, hessian = query_lambdas(
        doc_score[clipped], weight[clipped], jnp.where(usable, doc_label[clipped], 0), usable
    )
    target = jnp.where(usable, flat_index, doc_count).reshape(-1)
    grad_flat = (
        jnp.zeros((doc_count + 1,), jnp.float32).at[target].set(gradient.reshape(-1))[:doc_count]
    )
    hess_flat = (
        jnp.zeros((doc_count + 1,), jnp.float32).at[target].set(hessian.reshape(-1))[:doc_count]
    )
    return (grad_flat, hess_flat)


def bin_totals(left_rows, bin_index, anchor, feat_span, doc_block):
    block_count = left_rows.shape[1] // doc_block
    bin_ids = jnp.arange(BINS, dtype=jnp.int32)

    def add_block(counter, totals):
        offset = counter * doc_block
        sliced = lax.dynamic_slice_in_dim(left_rows, offset, doc_block, 1)
        bin_cells = lax.dynamic_slice(bin_index, (anchor, offset), (feat_span, doc_block))
        onehot = (bin_cells[:, :, None] == bin_ids[None, None, :]).astype(jnp.bfloat16)
        return totals + jnp.einsum(
            "nd,fdb->nfb", sliced, onehot, preferred_element_type=jnp.float32
        )

    totals = jnp.zeros((left_rows.shape[0], feat_span, BINS), jnp.float32)
    return lax.fori_loop(0, block_count, add_block, totals)


def all_features(left_rows, bin_index, feat_span, doc_block):
    feat_block = 4

    def fill_block(counter, stored):
        anchor = counter * feat_block
        partial_value = bin_totals(left_rows, bin_index, anchor, feat_block, doc_block)
        return lax.dynamic_update_slice_in_dim(stored, partial_value, anchor, 1)

    start_value = jnp.zeros((left_rows.shape[0], feat_span, BINS), jnp.float32)
    return lax.fori_loop(0, feat_span // feat_block, fill_block, start_value)


def local(
    scores,
    weights,
    labels,
    owner_row,
    owner_slot,
    query_len,
    bin_index,
    parent,
    split_feat,
    split_thr,
):
    doc_count = scores.shape[0]
    row_count = lax.axis_size("rows")
    feat_count = lax.axis_size("feat")
    slot_size = 2 * (doc_count // row_count)
    peer_ids = jnp.arange(row_count, dtype=jnp.int32)
    peer_hot = (owner_row[:, None] == peer_ids[None, :]).astype(jnp.int32)
    earlier = jnp.cumsum(peer_hot, axis=0) - peer_hot
    send_pos = jnp.sum(earlier * peer_hot, axis=1)
    outbound = jnp.zeros((row_count, 2, slot_size), jnp.float32)
    outbound = (
        outbound.at[owner_row, 0, send_pos].set(scores).at[owner_row, 1, send_pos].set(weights)
    )
    slot_codes = (
        jnp.full((row_count, slot_size), -1, jnp.int32)
        .at[owner_row, send_pos]
        .set(owner_slot * 8 + labels)
    )
    inbound, in_codes = (
        lax.all_to_all(outbound, "rows", split_axis=0, concat_axis=0, tiled=True),
        lax.all_to_all(slot_codes, "rows", split_axis=0, concat_axis=0, tiled=True),
    )
    filled = in_codes >= 0
    flat_slot = jnp.where(filled, in_codes // 8, doc_count)
    own_score = (
        jnp.zeros((doc_count + 1,), jnp.float32).at[flat_slot].set(inbound[:, 0, :])[:doc_count]
    )
    own_weight = (
        jnp.zeros((doc_count + 1,), jnp.float32).at[flat_slot].set(inbound[:, 1, :])[:doc_count]
    )
    own_label = jnp.zeros((doc_count + 1,), jnp.int32).at[flat_slot].set(in_codes % 8)[:doc_count]
    gradient, hessian = owner_lambdas(own_score, own_weight, own_label, query_len[0])
    fetch_slot = jnp.minimum(flat_slot, doc_count - 1)
    returned = jnp.stack([gradient[fetch_slot], hessian[fetch_slot]], axis=1)
    returned = jnp.where(filled[:, None, :], returned, 0.0).astype(jnp.bfloat16)
    arrived = lax.all_to_all(returned, "rows", split_axis=0, concat_axis=0, tiled=True)
    own_grads = jnp.stack(
        [arrived[owner_row, 0, send_pos], arrived[owner_row, 1, send_pos]], axis=0
    )
    feat_span = bin_index.shape[0]
    group_docs = bin_index.shape[1]
    column = lax.axis_index("feat")
    parent_hot = (parent[:, None] == jnp.arange(PARENTS, dtype=jnp.int32)[None, :]).astype(
        jnp.int32
    )
    chosen = jnp.sum(parent_hot * split_feat[None, :], axis=1) - column * feat_span
    threshold = jnp.sum(parent_hot * split_thr[None, :], axis=1)
    owned_here = (chosen >= 0) & (chosen < feat_span)
    picked = jnp.take_along_axis(bin_index, jnp.clip(chosen, 0, feat_span - 1)[None, :], axis=0)[0]
    right_bit = (owned_here & (picked > threshold)).astype(jnp.int32)
    word_count = (group_docs + 29) // 30
    padded = (
        jnp.zeros((word_count * 30,), jnp.int32)
        .at[:group_docs]
        .set(right_bit)
        .reshape(word_count, 30)
    )
    powers = jnp.power(jnp.int32(2), jnp.arange(30, dtype=jnp.int32))
    bit_words = jnp.sum(padded * powers[None, :], axis=1).astype(jnp.int32)
    all_words = lax.all_gather(bit_words, "feat", axis=0, tiled=True)
    group_grad = lax.all_gather(own_grads, "feat", axis=1, tiled=True)
    merged = jnp.sum(all_words.reshape(feat_count, word_count), axis=0)
    unpacked = (merged[:, None] // powers[None, :] % 2).reshape(-1)[:group_docs]
    new_node = 2 * parent + unpacked
    own_nodes = lax.dynamic_slice_in_dim(new_node, column * doc_count, doc_count)
    node_hot = (jnp.arange(NODES, dtype=jnp.int32)[:, None] == new_node[None, :]).astype(
        jnp.bfloat16
    )
    left_rows = jnp.concatenate(
        [node_hot * group_grad[0][None, :], node_hot * group_grad[1][None, :]], axis=0
    )
    doc_block = math.gcd(group_docs, 512)
    complete = all_features(left_rows, bin_index, feat_span, doc_block)
    histogram = lax.psum_scatter(complete, "rows", scatter_dimension=0, tiled=True)
    return (histogram, own_nodes)


def solution(mesh):
    placed = (
        P(("rows", "feat")),
        P(("rows", "feat")),
        P(("rows", "feat")),
        P(("rows", "feat")),
        P(("rows", "feat")),
        P(("rows", "feat"), None),
        P("feat", "rows"),
        P("rows"),
        P(),
        P(),
    )
    return jax.shard_map(
        local,
        mesh=mesh,
        in_specs=placed,
        out_specs=(P("rows", "feat", None), P(("rows", "feat"))),
        check_vma=False,
    )
```

profile of v0, /device:TPU:1, one launch (start us, length us, event | category | flops | bytes accessed | tf_op | source)
XLA Modules:
  0.0 434.9 jit_solution(15431009317612346709)
XLA Ops:
  11.0 11.3 %scatter_fusion = s32[64,8]{0,1:T(8,128)S(1)} fusion(s32[64,8]{0,1:T(8,128)S(1)} %broadcast_in_dim.43, s32[256]{0:T(256)S(1)} %bitcast.76, s32[256]{0:T(256)S(1)} %multiply_add_fusion), kind=kCustom, calls=%fused_computation.8 | custom fusion | bytes 5120 | tf_op jit(solution)/shard_map/scatter | solution.py:126
  23.0 11.6 %all-to-all-start = ((s32[64,1,8]{2,1,0:T(1,128)}), s32[64,1,8]{2,1,0:T(1,128)S(1)}, u32[]{:S(2)}, u32[]{:S(2)}) async-start(s32[64,1,8]{2,1,0:T(1,128)} %copy.41), calls=%async_computation | async-start | bytes 65536 | tf_op jit(solution)/shard_map/all_to_all | solution.py:130
  35.7 16.8 %gather_fusion.7 = s32[2048]{0:T(1024)S(1)} fusion(s32[64,2048]{1,0:T(8,128)S(1)} %copy-done, s32[2048]{0:T(1024)S(1)} %bitcast.73), kind=kCustom, calls=%fused_computation.7 | custom fusion | bytes 32768 | tf_op jit(solution)/shard_map/jit(take_along_axis)/gather | solution.py:158
  54.9 15.9 %all-reduce.1 = s32[552]{0:T(1024)S(1)} all-reduce(s32[552]{0:T(1024)S(1)} %dynamic-update-slice.2), channel_id=1, replica_groups=mesh['rows'=64,'feat'=8] {'feat'}, use_global_device_ids=true, to_apply=%add.1 | all-reduce | flops 552 | bytes 4416
  72.6 15.1 %scatter_fusion.1 = f32[64,2,8]{0,2,1:T(8,128)S(1)} fusion(f32[64,2,8]{0,2,1:T(8,128)S(1)} %broadcast_in_dim.51, s32[256]{0:T(256)S(1)} %bitcast.75, f32[256]{0:T(256)S(1)} %copy-done.3), kind=kCustom, calls=%fused_computation.10 | custom fusion | bytes 6144 | tf_op jit(solution)/shard_map/scatter | solution.py:121
  87.7 15.1 %scatter_fusion.2 = f32[64,2,8]{0,2,1:T(8,128)S(1)} fusion(f32[64,2,8]{0,2,1:T(8,128)S(1)} %scatter_fusion.1, s32[256]{0:T(256)S(1)} %bitcast.74, f32[256]{0:T(256)S(1)} %copy-done.4), kind=kCustom, calls=%fused_computation.11 | custom fusion | bytes 6144 | tf_op jit(solution)/shard_map/scatter | solution.py:121
  103.5 13.2 %all-to-all-start.1 = ((f32[64,2,8]{2,1,0:T(2,128)}), f32[64,2,8]{2,1,0:T(2,128)S(1)}, u32[]{:S(2)}, u32[]{:S(2)}) async-start(f32[64,2,8]{2,1,0:T(2,128)} %copy.43), calls=%async_computation.1 | async-start | bytes 131072 | tf_op jit(solution)/shard_map/all_to_all | solution.py:129
  119.6 3.5 gather_fusion
  131.9 3.5 gather_fusion.1
  135.4 3.5 gather_fusion.2
  148.4 3.4 gather_fusion.3
  152.8 7.5 %all-to-all-start.2 = ((bf16[64,2,8]{2,1,0:T(2,128)(2,1)}), bf16[64,2,8]{2,1,0:T(2,128)(2,1)S(1)}, u32[]{:S(2)}, u32[]{:S(2)}) async-start(bf16[64,2,8]{2,1,0:T(2,128)(2,1)} %copy.46), calls=%async_computation.2 | async-start | bytes 65536 | tf_op jit(solution)/shard_map/all_to_all | solution.py:145
  160.4 9.2 %all-to-all-done.2 = bf16[64,2,8]{2,1,0:T(2,128)(2,1)S(1)} async-done(((bf16[64,2,8]{2,1,0:T(2,128)(2,1)}), bf16[64,2,8]{2,1,0:T(2,128)(2,1)S(1)}, u32[]{:S(2)}, u32[]{:S(2)}) %all-to-all-start.2) | async-done | bytes 2080 | tf_op jit(solution)/shard_map/all_to_all | solution.py:145
  175.0 11.2 %all_gather.7 = bf16[2,2048]{1,0:T(2,128)(2,1)S(1)} all-gather(bf16[2,256]{1,0:T(2,128)(2,1)S(1)} %pad_maximum_fusion.1), channel_id=1, replica_groups=mesh['rows'=64,'feat'=8] {'feat'}, dimensions={1}, use_global_device_ids=true | all-gather | bytes 9216 | tf_op jit(solution)/shard_map/all_gather | solution.py:170
  188.7 96.6 %while.42 = (s32[]{:T(128)}, f32[64,64,256]{2,1,0:T(8,128)}, bf16[64,2048]{1,0:T(8,128)(2,1)S(1)}, s32[64,2048]{1,0:T(8,128)S(1)}, s32[]{:T(128)}, /*index=5*/s3...) while((s32[]{:T(128)}, f32[64,64,256]{2,1,0:T(8,128)}, ...), condition=%wide.region_26.27_spmd, body=%wide.region_23.26_spmd.sunk | while | flops 67764240 | bytes 1139616 | solution.py:96
  188.7 5.1 %while.43 = (s32[]{:T(128)}, f32[64,4,256]{2,0,1:T(8,128)S(1)}, bf16[64,2048]{1,0:T(8,128)(2,1)S(1)}, s32[64,2048]{1,0:T(8,128)S(1)}, s32[]{:T(128)}, /*index=5*/s32[]{:T(128)}, s32[]{:T(128)}, s32[]{:T(128)}, s32[]{:T(128)}) while((s32[]{:T(128)}, f32[64,4,256]{2,0,1:T(8,128)S(1)}, bf16[64,2048]{1,0:T(8,128)(2,1)S(1)}, ...), condition=%wide.region_25.25_spmd.clone, body=%wide.region_24.24_spmd.clone.sunk | while | flops 67764232 | bytes 614565 | solution.py:84
  194.7 5.1 %while.43 = (s32[]{:T(128)}, f32[64,4,256]{2,0,1:T(8,128)S(1)}, bf16[64,2048]{1,0:T(8,128)(2,1)S(1)}, s32[64,2048]{1,0:T(8,128)S(1)}, s32[]{:T(128)}, /*index=5*/s32[]{:T(128)}, s32[]{:T(128)}, s32[]{:T(128)}, s32[]{:T(128)}) while((s32[]{:T(128)}, f32[64,4,256]{2,0,1:T(8,128)S(1)}, bf16[64,2048]{1,0:T(8,128)(2,1)S(1)}, ...), condition=%wide.region_25.25_spmd.clone, body=%wide.region_24.24_spmd.clone.sunk | while | flops 67764232 | bytes 614565 | solution.py:84
  200.8 5.1 %while.43 = (s32[]{:T(128)}, f32[64,4,256]{2,0,1:T(8,128)S(1)}, bf16[64,2048]{1,0:T(8,128)(2,1)S(1)}, s32[64,2048]{1,0:T(8,128)S(1)}, s32[]{:T(128)}, /*index=5*/s32[]{:T(128)}, s32[]{:T(128)}, s32[]{:T(128)}, s32[]{:T(128)}) while((s32[]{:T(128)}, f32[64,4,256]{2,0,1:T(8,128)S(1)}, bf16[64,2048]{1,0:T(8,128)(2,1)S(1)}, ...), condition=%wide.region_25.25_spmd.clone, body=%wide.region_24.24_spmd.clone.sunk | while | flops 67764232 | bytes 614565 | solution.py:84
  206.8 5.1 %while.43 = (s32[]{:T(128)}, f32[64,4,256]{2,0,1:T(8,128)S(1)}, bf16[64,2048]{1,0:T(8,128)(2,1)S(1)}, s32[64,2048]{1,0:T(8,128)S(1)}, s32[]{:T(128)}, /*index=5*/s32[]{:T(128)}, s32[]{:T(128)}, s32[]{:T(128)}, s32[]{:T(128)}) while((s32[]{:T(128)}, f32[64,4,256]{2,0,1:T(8,128)S(1)}, bf16[64,2048]{1,0:T(8,128)(2,1)S(1)}, ...), condition=%wide.region_25.25_spmd.clone, body=%wide.region_24.24_spmd.clone.sunk | while | flops 67764232 | bytes 614565 | solution.py:84
  212.9 5.1 %while.43 = (s32[]{:T(128)}, f32[64,4,256]{2,0,1:T(8,128)S(1)}, bf16[64,2048]{1,0:T(8,128)(2,1)S(1)}, s32[64,2048]{1,0:T(8,128)S(1)}, s32[]{:T(128)}, /*index=5*/s32[]{:T(128)}, s32[]{:T(128)}, s32[]{:T(128)}, s32[]{:T(128)}) while((s32[]{:T(128)}, f32[64,4,256]{2,0,1:T(8,128)S(1)}, bf16[64,2048]{1,0:T(8,128)(2,1)S(1)}, ...), condition=%wide.region_25.25_spmd.clone, body=%wide.region_24.24_spmd.clone.sunk | while | flops 67764232 | bytes 614565 | solution.py:84
  218.9 5.1 %while.43 = (s32[]{:T(128)}, f32[64,4,256]{2,0,1:T(8,128)S(1)}, bf16[64,2048]{1,0:T(8,128)(2,1)S(1)}, s32[64,2048]{1,0:T(8,128)S(1)}, s32[]{:T(128)}, /*index=5*/s32[]{:T(128)}, s32[]{:T(128)}, s32[]{:T(128)}, s32[]{:T(128)}) while((s32[]{:T(128)}, f32[64,4,256]{2,0,1:T(8,128)S(1)}, bf16[64,2048]{1,0:T(8,128)(2,1)S(1)}, ...), condition=%wide.region_25.25_spmd.clone, body=%wide.region_24.24_spmd.clone.sunk | while | flops 67764232 | bytes 614565 | solution.py:84
  225.0 5.1 %while.43 = (s32[]{:T(128)}, f32[64,4,256]{2,0,1:T(8,128)S(1)}, bf16[64,2048]{1,0:T(8,128)(2,1)S(1)}, s32[64,2048]{1,0:T(8,128)S(1)}, s32[]{:T(128)}, /*index=5*/s32[]{:T(128)}, s32[]{:T(128)}, s32[]{:T(128)}, s32[]{:T(128)}) while((s32[]{:T(128)}, f32[64,4,256]{2,0,1:T(8,128)S(1)}, bf16[64,2048]{1,0:T(8,128)(2,1)S(1)}, ...), condition=%wide.region_25.25_spmd.clone, body=%wide.region_24.24_spmd.clone.sunk | while | flops 67764232 | bytes 614565 | solution.py:84
  231.0 5.1 %while.43 = (s32[]{:T(128)}, f32[64,4,256]{2,0,1:T(8,128)S(1)}, bf16[64,2048]{1,0:T(8,128)(2,1)S(1)}, s32[64,2048]{1,0:T(8,128)S(1)}, s32[]{:T(128)}, /*index=5*/s32[]{:T(128)}, s32[]{:T(128)}, s32[]{:T(128)}, s32[]{:T(128)}) while((s32[]{:T(128)}, f32[64,4,256]{2,0,1:T(8,128)S(1)}, bf16[64,2048]{1,0:T(8,128)(2,1)S(1)}, ...), condition=%wide.region_25.25_spmd.clone, body=%wide.region_24.24_spmd.clone.sunk | while | flops 67764232 | bytes 614565 | solution.py:84
  237.1 5.1 %while.43 = (s32[]{:T(128)}, f32[64,4,256]{2,0,1:T(8,128)S(1)}, bf16[64,2048]{1,0:T(8,128)(2,1)S(1)}, s32[64,2048]{1,0:T(8,128)S(1)}, s32[]{:T(128)}, /*index=5*/s32[]{:T(128)}, s32[]{:T(128)}, s32[]{:T(128)}, s32[]{:T(128)}) while((s32[]{:T(128)}, f32[64,4,256]{2,0,1:T(8,128)S(1)}, bf16[64,2048]{1,0:T(8,128)(2,1)S(1)}, ...), condition=%wide.region_25.25_spmd.clone, body=%wide.region_24.24_spmd.clone.sunk | while | flops 67764232 | bytes 614565 | solution.py:84
  243.1 5.1 %while.43 = (s32[]{:T(128)}, f32[64,4,256]{2,0,1:T(8,128)S(1)}, bf16[64,2048]{1,0:T(8,128)(2,1)S(1)}, s32[64,2048]{1,0:T(8,128)S(1)}, s32[]{:T(128)}, /*index=5*/s32[]{:T(128)}, s32[]{:T(128)}, s32[]{:T(128)}, s32[]{:T(128)}) while((s32[]{:T(128)}, f32[64,4,256]{2,0,1:T(8,128)S(1)}, bf16[64,2048]{1,0:T(8,128)(2,1)S(1)}, ...), condition=%wide.region_25.25_spmd.clone, body=%wide.region_24.24_spmd.clone.sunk | while | flops 67764232 | bytes 614565 | solution.py:84
  249.2 5.1 %while.43 = (s32[]{:T(128)}, f32[64,4,256]{2,0,1:T(8,128)S(1)}, bf16[64,2048]{1,0:T(8,128)(2,1)S(1)}, s32[64,2048]{1,0:T(8,128)S(1)}, s32[]{:T(128)}, /*index=5*/s32[]{:T(128)}, s32[]{:T(128)}, s32[]{:T(128)}, s32[]{:T(128)}) while((s32[]{:T(128)}, f32[64,4,256]{2,0,1:T(8,128)S(1)}, bf16[64,2048]{1,0:T(8,128)(2,1)S(1)}, ...), condition=%wide.region_25.25_spmd.clone, body=%wide.region_24.24_spmd.clone.sunk | while | flops 67764232 | bytes 614565 | solution.py:84
  255.2 5.1 %while.43 = (s32[]{:T(128)}, f32[64,4,256]{2,0,1:T(8,128)S(1)}, bf16[64,2048]{1,0:T(8,128)(2,1)S(1)}, s32[64,2048]{1,0:T(8,128)S(1)}, s32[]{:T(128)}, /*index=5*/s32[]{:T(128)}, s32[]{:T(128)}, s32[]{:T(128)}, s32[]{:T(128)}) while((s32[]{:T(128)}, f32[64,4,256]{2,0,1:T(8,128)S(1)}, bf16[64,2048]{1,0:T(8,128)(2,1)S(1)}, ...), condition=%wide.region_25.25_spmd.clone, body=%wide.region_24.24_spmd.clone.sunk | while | flops 67764232 | bytes 614565 | solution.py:84
  261.2 5.1 %while.43 = (s32[]{:T(128)}, f32[64,4,256]{2,0,1:T(8,128)S(1)}, bf16[64,2048]{1,0:T(8,128)(2,1)S(1)}, s32[64,2048]{1,0:T(8,128)S(1)}, s32[]{:T(128)}, /*index=5*/s32[]{:T(128)}, s32[]{:T(128)}, s32[]{:T(128)}, s32[]{:T(128)}) while((s32[]{:T(128)}, f32[64,4,256]{2,0,1:T(8,128)S(1)}, bf16[64,2048]{1,0:T(8,128)(2,1)S(1)}, ...), condition=%wide.region_25.25_spmd.clone, body=%wide.region_24.24_spmd.clone.sunk | while | flops 67764232 | bytes 614565 | solution.py:84
  267.2 5.1 %while.43 = (s32[]{:T(128)}, f32[64,4,256]{2,0,1:T(8,128)S(1)}, bf16[64,2048]{1,0:T(8,128)(2,1)S(1)}, s32[64,2048]{1,0:T(8,128)S(1)}, s32[]{:T(128)}, /*index=5*/s32[]{:T(128)}, s32[]{:T(128)}, s32[]{:T(128)}, s32[]{:T(128)}) while((s32[]{:T(128)}, f32[64,4,256]{2,0,1:T(8,128)S(1)}, bf16[64,2048]{1,0:T(8,128)(2,1)S(1)}, ...), condition=%wide.region_25.25_spmd.clone, body=%wide.region_24.24_spmd.clone.sunk | while | flops 67764232 | bytes 614565 | solution.py:84
  273.3 5.1 %while.43 = (s32[]{:T(128)}, f32[64,4,256]{2,0,1:T(8,128)S(1)}, bf16[64,2048]{1,0:T(8,128)(2,1)S(1)}, s32[64,2048]{1,0:T(8,128)S(1)}, s32[]{:T(128)}, /*index=5*/s32[]{:T(128)}, s32[]{:T(128)}, s32[]{:T(128)}, s32[]{:T(128)}) while((s32[]{:T(128)}, f32[64,4,256]{2,0,1:T(8,128)S(1)}, bf16[64,2048]{1,0:T(8,128)(2,1)S(1)}, ...), condition=%wide.region_25.25_spmd.clone, body=%wide.region_24.24_spmd.clone.sunk | while | flops 67764232 | bytes 614565 | solution.py:84
  279.3 5.1 %while.43 = (s32[]{:T(128)}, f32[64,4,256]{2,0,1:T(8,128)S(1)}, bf16[64,2048]{1,0:T(8,128)(2,1)S(1)}, s32[64,2048]{1,0:T(8,128)S(1)}, s32[]{:T(128)}, /*index=5*/s32[]{:T(128)}, s32[]{:T(128)}, s32[]{:T(128)}, s32[]{:T(128)}) while((s32[]{:T(128)}, f32[64,4,256]{2,0,1:T(8,128)S(1)}, bf16[64,2048]{1,0:T(8,128)(2,1)S(1)}, ...), condition=%wide.region_25.25_spmd.clone, body=%wide.region_24.24_spmd.clone.sunk | while | flops 67764232 | bytes 614565 | solution.py:84
  286.0 142.0 %reduce-scatter.2.cloned.1.call-done = f32[1,64,256]{2,1,0:T(8,128)} async-done(((f32[64,64,256]{2,1,0:T(8,128)}), f32[1,64,256]{2,1,0:T(8,128)}) %reduce-scatter.2.cloned.1.call-update) | async-done | bytes 65552 | tf_op jit(solution)/shard_map/reduce_scatter | solution.py:183
  (269 shorter events, 135.2 us)
Async XLA Ops:
  7.2 28.4 %copy-start = (s32[64,2048]{1,0:T(8,128)S(1)}, s32[64,2048]{1,0:T(8,128)}, u32[]{:S(2)}) copy-start(s32[64,2048]{1,0:T(8,128)} %param.22) | copy-start | bytes 1572868
  23.0 80.5 %all-to-all-start = ((s32[64,1,8]{2,1,0:T(1,128)}), s32[64,1,8]{2,1,0:T(1,128)S(1)}, u32[]{:S(2)}, u32[]{:S(2)}) async-start(s32[64,1,8]{2,1,0:T(1,128)} %copy.41), calls=%async_computation | async-start | bytes 65536 | tf_op jit(solution)/shard_map/all_to_all | solution.py:130
  35.6 36.6 %copy-start.2 = (s32[1,4]{1,0:T(1,128)S(1)}, s32[1,4]{1,0:T(1,128)}, u32[]{:S(2)}) copy-start(s32[1,4]{1,0:T(1,128)} %param.21) | copy-start | bytes 52
  35.6 37.0 %copy-start.3 = (f32[256]{0:T(256)S(1)}, f32[256]{0:T(256)}, u32[]{:S(2)}) copy-start(f32[256]{0:T(256)} %param.16) | copy-start | bytes 3076
  35.6 52.0 %copy-start.4 = (f32[256]{0:T(256)S(1)}, f32[256]{0:T(256)}, u32[]{:S(2)}) copy-start(f32[256]{0:T(256)} %param.17) | copy-start | bytes 3076
  103.5 23.0 %all-to-all-start.1 = ((f32[64,2,8]{2,1,0:T(2,128)}), f32[64,2,8]{2,1,0:T(2,128)S(1)}, u32[]{:S(2)}, u32[]{:S(2)}) async-start(f32[64,2,8]{2,1,0:T(2,128)} %copy.43), calls=%async_computation.1 | async-start | bytes 131072 | tf_op jit(solution)/shard_map/all_to_all | solution.py:129
  148.4 12.0 %copy-start.1 = (s32[2048]{0:T(1024)S(1)}, s32[2048]{0:T(1024)}, u32[]{:S(2)}) copy-start(s32[2048]{0:T(1024)} %param.23) | copy-start | bytes 24580
  152.8 16.7 %all-to-all-start.2 = ((bf16[64,2,8]{2,1,0:T(2,128)(2,1)}), bf16[64,2,8]{2,1,0:T(2,128)(2,1)S(1)}, u32[]{:S(2)}, u32[]{:S(2)}) async-start(bf16[64,2,8]{2,1,0:T(2,128)(2,1)} %copy.46), calls=%async_computation.2 | async-start | bytes 65536 | tf_op jit(solution)/shard_map/all_to_all | solution.py:145
  160.3 267.7 %reduce-scatter.2.cloned.1.call-start = ((), (), s32[]{:S(2)}) async-start(), calls=%async_computation.4 | async-start | bytes 4259840 | tf_op jit(solution)/shard_map/reduce_scatter | solution.py:183
Sparse Core Ops, SparseCore 0:
  285.4 142.5 reduce-scatter.1
where the time goes:
time: 439 us; the launch traced here: 435 us
  waiting for transfers between devices  154 us (35%)
  local copies, waits for them, and re-layouts  122 us (28%)
  matrix products  74.8 us (17%)
  starting transfers between devices  32.3 us (7%)
  blocking collectives  27.1 us (6%)
  between operations  15.2 us (3%)
  other arithmetic  7.76 us (2%)
    reduce_scatter x1, waiting for transfers between devices, local(): lax.psum_scatter(complete, 'rows', scatter_dimension=0, tiled=True)  142 us
    dot_general x64, matrix products, add_block(): jnp.einsum('nd,fdb->nfb', sliced, onehot, preferred_element_type=jnp.floa...  74.8 us
    scatter x3, local copies, waits for them, and re-layouts, local(): outbound.at[owner_row, 0, send_pos].set(scores).at[owner_row, 1, send_pos]  30.8 us
    gather x1, local copies, waits for them, and re-layouts, local(): jnp.take_along_axis(bin_index, jnp.clip(chosen, 0, feat_span - 1)[None, :...  16.8 us
    unnamed x1, blocking collectives  15.9 us
    dynamic_update_slice x16, local copies, waits for them, and re-layouts, fill_block(): return lax.dynamic_update_slice_in_dim(stored, partial_value, anchor, 1)  14.8 us
    all_to_all x1, starting transfers between devices, local(): lax.all_to_all(outbound, 'rows', split_axis=0, concat_axis=0, tiled=True)  13.2 us
    all_to_all x1, starting transfers between devices, local(): lax.all_to_all(slot_codes, 'rows', split_axis=0, concat_axis=0, tiled=True)  11.6 us
  transfers between devices with their start and end apart: 4, of which 3 were waited for; matrix products, arithmetic and copies ran while one was open for 14% of the time, Pallas kernels for 0%

commit v1 on v0

v1 whole, which is shorter than its diff:
```python
import functools

import jax
import jax.numpy as jnp
from jax import lax
from jax.experimental import pallas as pl
from jax.experimental.pallas import tpu as pltpu
from jax.sharding import PartitionSpec as P

BINS = 256
NODES = 32
QMAX = 128
PARENTS = 16
ROWS = 64
FEATS = 8
DOC = 256
GROUP = FEATS * DOC
SPAN = 64
CAP = 160
SLOTS = PARENTS * CAP
POS = 8
PEERS = 16
TAKEN = PEERS * CAP
TILES = TAKEN // 128
CHUNK = 88
SHARE = 64

F32 = jnp.float32
BF16 = jnp.bfloat16
I32 = jnp.int32


def iota(shape, dim):
    return lax.broadcasted_iota(I32, shape, dim)


def nt(a, b):
    return lax.dot_general(a, b, (((1,), (1,)), ((), ())), preferred_element_type=F32)


def nn(a, b):
    return jnp.dot(a, b, preferred_element_type=F32)


def as_hot(mask):
    return jnp.where(mask, 1.0, 0.0).astype(BF16)


def three_parts(x):
    top = x.astype(BF16).astype(F32)
    rest = x - top
    middle = rest.astype(BF16).astype(F32)
    return top, middle, rest - middle


def swap_matrix():
    row = iota((512, 1), 0)
    goal = ((row >> 5) & 3) * 128 + (row >> 7) * 32 + (row & 31)
    return as_hot(goal == iota((512, 512), 1))


def earlier_matrix():
    return as_hot(iota((DOC, DOC), 0) < iota((DOC, DOC), 1))


def stack_rows(rows, height, width):
    place = iota((height, width), 0)
    out = jnp.zeros((height, width), F32)
    for at, row in enumerate(rows):
        out = jnp.where(place == at, row, out)
    return out


def send_kernel(score_ref, weight_ref, label_ref, owner_ref, slot_ref, out_ref):
    owner = owner_ref[...]
    hot = jnp.where(iota((ROWS, DOC), 0) == owner, 1.0, 0.0)
    before = nn(hot.astype(BF16), earlier_matrix())
    place = jnp.sum(hot * before, axis=0, keepdims=True)
    rows = [
        *three_parts(score_ref[...]),
        *three_parts(weight_ref[...]),
        slot_ref[...].astype(F32) + 1.0,
        label_ref[...].astype(F32),
    ]
    values = stack_rows(rows, 16, DOC)
    tiled = jnp.concatenate([values] * POS, axis=0)
    group = iota((16 * POS, DOC), 0) >> 4
    total = jnp.zeros((ROWS, 128), F32)
    for pos in range(POS):
        here = jnp.where(place == float(pos), hot, 0.0).astype(BF16)
        total += nt(here, jnp.where(group == pos, tiled, 0.0).astype(BF16))
    out_ref[:, 0, :] = total


def owner_kernel(len_ref, in_ref, out_ref):
    data = in_ref[:, 0, :]
    turned = jnp.transpose(data).astype(BF16)
    lane = iota((ROWS, DOC), 1).astype(F32) + 1.0
    table = jnp.zeros((16, DOC), F32)
    for pos in range(POS):
        hot = as_hot(data[:, pos * 16 + 6 : pos * 16 + 7] == lane)
        table += nn(turned[pos * 16 : pos * 16 + 16, :], hot)
    same = as_hot(iota((DOC, DOC), 0) == iota((DOC, DOC), 1))
    upright = nt(same, table.astype(BF16))
    s_j = table[0:1] + table[1:2] + table[2:3]
    w_j = table[3:4] + table[4:5] + table[5:6]
    l_j = table[7:8]
    s_i = upright[:, 0:1] + upright[:, 1:2] + upright[:, 2:3]
    w_i = upright[:, 3:4] + upright[:, 4:5] + upright[:, 5:6]
    l_i = upright[:, 7:8]

    ends = []
    total = 0
    for q in range(3):
        total = total + len_ref[0, q]
        ends.append(total)

    def query_of(at):
        return sum([(at >= end).astype(I32) for end in ends])

    def gain(label):
        return sum([jnp.where(label >= float(l), 2.0 ** (l - 1), 0.0) for l in range(1, 5)])

    row_at = iota((1, DOC), 1)
    q_j = query_of(row_at)
    q_i = query_of(iota((DOC, 1), 0))
    n_j = jnp.zeros((1, DOC), F32)
    for q in range(4):
        n_j = jnp.where(q_j == q, len_ref[0, q].astype(F32), n_j)

    case = iota((16, DOC), 0)
    level = ((case & 3) + 1).astype(F32)
    reaches = (q_j == (case >> 2)) & (l_j >= level)
    count = jnp.sum(jnp.where(reaches, 1.0, 0.0), axis=1, keepdims=True)
    spot = iota((16, QMAX), 1).astype(F32)
    step = jnp.left_shift(1, iota((16, QMAX), 0) & 3).astype(F32)
    share = jnp.where(spot < count, step * (0.6931471805599453 / jnp.log(spot + 2.0)), 0.0)
    share = jnp.sum(share, axis=1, keepdims=True)
    ideal = jnp.sum(jnp.where(q_j == (case >> 2), share, 0.0), axis=0, keepdims=True)
    inverse = 1.0 / jnp.maximum(ideal, 1.0)

    mate = q_i == q_j
    earlier = iota((DOC, DOC), 1) < iota((DOC, DOC), 0)
    above = mate & ((s_j > s_i) | ((s_j == s_i) & earlier))
    above = jnp.where(above, 1.0, 0.0)
    rank_i = 1.0 + jnp.sum(above, axis=1, keepdims=True)
    rank_j = n_j - jnp.sum(above, axis=0, keepdims=True)
    disc_i = 0.6931471805599453 / jnp.log(1.0 + rank_i)
    disc_j = 0.6931471805599453 / jnp.log(1.0 + rank_j)
    step_gain = gain(l_i) - gain(l_j)
    odds = jnp.exp(s_i - s_j)
    miss = 1.0 / (1.0 + odds)
    swap = jnp.where(mate, jnp.abs(disc_i - disc_j) * w_i, 0.0) * miss
    push = swap * step_gain * jnp.where(step_gain > 0.0, 1.0, odds)
    bend = swap * jnp.abs(step_gain) * (odds * miss)
    scale = w_j * inverse
    grad = jnp.sum(push, axis=0, keepdims=True) * scale
    hess = jnp.sum(bend, axis=0, keepdims=True) * scale
    grad = grad.astype(BF16).astype(F32)
    hess = hess.astype(BF16).astype(F32)
    both = jnp.concatenate([grad, hess], axis=0)
    out_ref[...] = jnp.broadcast_to(both.reshape(1, 2, DOC), (ROWS, 2, DOC))


def sort_kernel(
    feat_ref, thr_ref, col_ref, parent_ref, bins_ref, owner_ref, slot_ref, out_ref, bits_ref, fold_ref, left_ref
):
    column = col_ref[0]
    parent = parent_ref[...]
    hot = jnp.where(iota((PARENTS, GROUP), 0) == parent, 1.0, 0.0)
    hot_b = hot.astype(BF16)
    earlier = earlier_matrix()
    carry = jnp.zeros((PARENTS, 1), F32)
    ranks = []
    for block in range(FEATS):
        part = hot[:, block * DOC : (block + 1) * DOC]
        before = nn(hot_b[:, block * DOC : (block + 1) * DOC], earlier) + carry
        ranks.append(jnp.sum(part * before, axis=0, keepdims=True))
        carry = carry + jnp.sum(part, axis=1, keepdims=True)
    target = parent.astype(F32) * float(CAP) + jnp.concatenate(ranks, axis=1)

    bits = jnp.zeros((1, GROUP), F32)
    for p in range(PARENTS):
        at = feat_ref[p] - column * SPAN
        here = jnp.where((at >= 0) & (at < SPAN), 1.0, 0.0)
        row = bins_ref[pl.ds(jnp.clip(at, 0, SPAN - 1), 1), :]
        right = (parent == p) & (row > thr_ref[p])
        bits = bits + jnp.where(right, here, 0.0)
    bits_ref[...] = bits

    own = (iota((1, GROUP), 1) >> 8) == column
    owner = jnp.concatenate([owner_ref[...].astype(F32) + 1.0] * FEATS, axis=1)
    slot = jnp.concatenate([slot_ref[...].astype(F32)] * FEATS, axis=1)
    left_ref[0:SPAN, :] = bins_ref[...].astype(F32).astype(BF16)
    extra = [jnp.where(own, owner, 0.0), jnp.where(own, slot, 0.0), bits, jnp.zeros_like(bits)]
    for q in range(4):
        left_ref[SPAN + q * 16 : SPAN + q * 16 + 16, :] = jnp.broadcast_to(extra[q], (16, GROUP)).astype(BF16)

    left = left_ref[...]
    line = iota((256, GROUP), 0).astype(F32)
    for pair in range(SLOTS // 256):
        pick = as_hot(line == (target - float(256 * pair)))
        got = nt(left, pick).astype(BF16)
        for half in range(2):
            t = pair * 2 + half
            for q in range(4):
                lanes = slice(q * 128, q * 128 + 128)
                cols = slice(half * 128, half * 128 + 128)
                fold_ref[t * 16 : t * 16 + 16, lanes] = got[q * 16 : q * 16 + 16, cols]
                fold_ref[320 + t * 16 : 336 + t * 16, lanes] = got[64 + q * 16 : 80 + q * 16, cols]
    folded = nn(fold_ref[...], swap_matrix())
    which = iota((16, 128), 0)
    for p in range(PARENTS):
        tail = jnp.zeros((16, 128), F32)
        for g in range(5):
            t, a = divmod(p * 5 + g, 4)
            block = folded[t * 16 : t * 16 + 16, a * 128 : a * 128 + 128].astype(BF16)
            out_ref[p, g * 16 : g * 16 + 16, :] = block
            tail = jnp.where(which == g, folded[320 + t * 16 : 336 + t * 16, a * 128 : a * 128 + 128], tail)
        out_ref[p, 80:88, :] = tail[0:8].astype(BF16)


def open_kernel(in_ref, bins_ref, extra_ref):
    swap = swap_matrix()
    for r in range(PEERS // 4):
        four = jnp.concatenate([in_ref[4 * r + a] for a in range(4)], axis=1)
        flat = nn(four, swap)
        for g in range(5):
            t = r * 5 + g
            for q in range(4):
                bins_ref[q * 16 : q * 16 + 16, t * 128 : t * 128 + 128] = flat[
                    g * 16 : g * 16 + 16, q * 128 : q * 128 + 128
                ].astype(BF16)
        for q in range(3):
            extra_ref[q, r] = flat[80:88, q * 128 : q * 128 + 128]


def pick_kernel(grads_ref, extra_ref, bits_ref, out_ref, all_ref):
    turned = jnp.concatenate([jnp.transpose(grads_ref[:, k, :]) for k in range(2)], axis=0)
    turned = turned.astype(BF16)
    owner_line = (iota((ROWS, 128), 0) + 1).astype(F32)
    slot_line = iota((DOC, 128), 0).astype(F32)
    for t in range(TILES):
        r, g = divmod(t, 5)
        owner = extra_ref[0, r, g : g + 1, :]
        slot = extra_ref[1, r, g : g + 1, :]
        from_owner = nn(turned, as_hot(owner_line == owner))
        hit = slot_line == slot
        for k in range(2):
            mine = jnp.where(hit, from_owner[k * DOC : k * DOC + DOC], 0.0)
            all_ref[k * TILES + t : k * TILES + t + 1, :] = jnp.sum(mine, axis=0, keepdims=True)
        all_ref[2 * TILES + t : 2 * TILES + t + 1, :] = extra_ref[2, r, g : g + 1, :]
    all_ref[62:64, :] = jnp.zeros((2, 128), F32)
    for c in range(FEATS):
        all_ref[60:62, :] = bits_ref[2 * c : 2 * c + 2, :]
        out_ref[c] = all_ref[...].astype(BF16)


def histogram_kernel(col_ref, shares_ref, bins_ref, parent_ref, out_ref, node_ref, sums_ref, vals_ref):
    sums = shares_ref[0].astype(F32)
    for c in range(1, FEATS):
        sums = sums + shares_ref[c].astype(F32)
    sums_ref[...] = sums
    node_ref[...] = 2 * parent_ref[pl.ds(2 * col_ref[0], 2), :] + sums_ref[60:62, :].astype(I32)

    child = (iota((16, 128), 0) >> 3).astype(F32)
    for t in range(TILES):
        bit = sums_ref[2 * TILES + t : 2 * TILES + t + 1, :]
        for k in range(2):
            value = sums_ref[k * TILES + t : k * TILES + t + 1, :]
            vals_ref[k * 16 : k * 16 + 16, t * 128 : t * 128 + 128] = jnp.where(
                child == bit, value, 0.0
            ).astype(BF16)

    vals = [vals_ref[0:16, :], vals_ref[16:32, :]]
    zero = jnp.zeros((16, TAKEN), BF16)
    one = jnp.ones((16, TAKEN), BF16)
    odd = iota((16, TAKEN), 0) >> 3
    row = iota((256, 256), 0)
    lane = iota((256, 256), 1)
    own = (row & 7) == (lane & 7)
    fold = as_hot((row >> 3) == (lane & 31))
    block = iota((32, 256), 1) >> 5
    for g in range(SPAN // 8):
        bins = bins_ref[g // 2 * 16 : g // 2 * 16 + 16, :].astype(F32)
        bins = bins[g % 2 * 8 : g % 2 * 8 + 8, :]
        high = jnp.floor(bins * (1.0 / 32.0))
        low = bins - high * 32.0
        high = jnp.concatenate([high, high], axis=0).astype(BF16)
        low = (jnp.concatenate([low, low], axis=0) - odd.astype(F32)).astype(BF16)
        tall = []
        for h in range(8):
            hit = high == jnp.array(h, BF16)
            tall += [jnp.where(hit, v, zero) for v in vals]
        flat = [jnp.where(low == jnp.array(2 * l, BF16), one, zero) for l in range(16)]
        acc = nt(jnp.concatenate(tall, axis=0), jnp.concatenate(flat, axis=0))
        parts = three_parts(jnp.where(own, acc, 0.0))
        wide = sum([nn(part.astype(BF16), fold) for part in parts])
        total = jnp.zeros((32, 256), F32)
        for h in range(8):
            total = jnp.where(block == h, wide[h * 32 : h * 32 + 32, :], total)
        for k in range(4):
            out_ref[k, g * 8 : g * 8 + 8, :] = total[k * 8 : k * 8 + 8, :]


SMEM = pl.BlockSpec(memory_space=pltpu.SMEM)
VMEM = pl.BlockSpec(memory_space=pltpu.VMEM)


def call(kernel, ins, outs, scratch=(), **more):
    return pl.pallas_call(
        kernel,
        out_shape=[jax.ShapeDtypeStruct(s, d) for s, d in outs],
        in_specs=list(ins),
        out_specs=[VMEM] * len(outs),
        scratch_shapes=list(scratch),
        **more,
    )


def exchange(x, **more):
    return lax.all_to_all(x, "rows", split_axis=0, concat_axis=0, tiled=True, **more)


def local(
    scores, weights, labels, owner_row, owner_slot, query_len, bin_index, parent, split_feat, split_thr
):
    column = lax.axis_index("feat").astype(I32).reshape(1)
    classes = [[32 * h + 2 * i + k for i in range(PEERS)] for h in range(2) for k in range(2)]
    quads = [[2 * p, 2 * p + 1, 32 + 2 * p, 33 + 2 * p] for p in range(PARENTS)]

    def line(x):
        return x.reshape(1, DOC)

    (outbound,) = call(send_kernel, [VMEM] * 5, [((ROWS, 1, 128), F32)])(
        line(scores), line(weights), line(labels), line(owner_row), line(owner_slot)
    )
    inbound = exchange(outbound)
    sorted_docs, bits = call(
        sort_kernel,
        [SMEM] * 3 + [VMEM] * 4,
        [((PEERS, CHUNK, 128), BF16), ((1, GROUP), F32)],
        [pltpu.VMEM((640, 512), BF16), pltpu.VMEM((128, GROUP), BF16)],
    )(
        split_feat,
        split_thr,
        column,
        parent.reshape(1, GROUP),
        bin_index,
        line(owner_row),
        line(owner_slot),
    )
    taken = exchange(sorted_docs, axis_index_groups=classes)
    (spread,) = call(owner_kernel, [SMEM, VMEM], [((ROWS, 2, DOC), F32)])(query_len, inbound)
    grads = exchange(spread)
    bins, extra = call(
        open_kernel, [VMEM], [((SPAN, TAKEN), BF16), ((3, PEERS // 4, 8, 128), F32)]
    )(taken)
    (share,) = call(
        pick_kernel, [VMEM] * 3, [((FEATS, SHARE, 128), BF16)], [pltpu.VMEM((SHARE, 128), F32)]
    )(grads, extra, bits.reshape(16, 128))
    shares = lax.all_to_all(share, "feat", split_axis=0, concat_axis=0, tiled=True)
    rows, new_node = call(
        histogram_kernel,
        [SMEM] + [VMEM] * 3,
        [((4, SPAN, BINS), F32), ((2, 128), I32)],
        [pltpu.VMEM((SHARE, 128), F32), pltpu.VMEM((32, TAKEN), BF16)],
    )(column, shares, bins, parent.reshape(16, 128))
    came = exchange(rows, axis_index_groups=quads)
    return (jnp.sum(came, axis=0, keepdims=True), new_node.reshape(DOC))


def solution(mesh):
    docs = P(("rows", "feat"))
    placed = (docs,) * 5 + (P(("rows", "feat"), None), P("feat", "rows"), P("rows"), P(), P())
    return jax.shard_map(
        local,
        mesh=mesh,
        in_specs=placed,
        out_specs=(P("rows", "feat", None), docs),
        check_vma=False,
    )
```

time: 439 us -> 102 us (0.23)
  waiting for transfers between devices: 154 us -> 19.2 us
  local copies, waits for them, and re-layouts: 122 us -> 1.27 us
  matrix products: 74.8 us -> 0 us
  Pallas kernels: 0 us -> 24.6 us
  between operations: 15.2 us -> 0.67 us
  other arithmetic: 7.76 us -> 0.65 us
  starting transfers between devices: 32.3 us -> 25.3 us
    reduce_scatter x1 -> x0, waiting for transfers between devices: 142 us -> none  [local(): lax.psum_scatter(complete, 'rows', scatter_dimension=0, tiled=True)]
    dot_general x64 -> x0, matrix products: 74.8 us -> none  [add_block(): jnp.einsum('nd,fdb->nfb', sliced, onehot, preferred_element_type=jnp.floa...]
    scatter x10 -> x0, local copies, waits for them, and re-layouts: 54.5 us -> none  [the longest x3 30.8 us: local(): outbound.at[owner_row, 0, send_pos].set(scores).at[owner_row, 1, send_pos]]
    gather x8 -> x0, local copies, waits for them, and re-layouts: 39.3 us -> none  [the longest x1 16.8 us: local(): jnp.take_along_axis(bin_index, jnp.clip(chosen, 0, feat_span - 1)[None, :...]
    all_to_all x0 -> x2, blocking collectives: none -> 30 us  [the longest x1 18 us: local(): lax.all_to_all(share, 'feat', split_axis=0, concat_axis=0, tiled=True)]
    pallas_call x0 -> x6, Pallas kernels: none -> 24.6 us  [the longest x1 9.15 us: local(): call(histogram_kernel, [SMEM] + [VMEM] * 3, [((4, SPAN, BINS), F32), ((2,...]
    unnamed x1 -> x0, blocking collectives: 15.9 us -> none
    dynamic_update_slice x16 -> x0, local copies, waits for them, and re-layouts: 14.8 us -> none  [fill_block(): return lax.dynamic_update_slice_in_dim(stored, partial_value, anchor, 1)]
  transfers between devices with their start and end apart: 4 -> 3, of which waited for: 3 -> 3; matrix products, arithmetic and copies ran while one was open for 14% -> 0% of each run, Pallas kernels for 0% -> 11%
where the time goes in v1:
time: 102 us
  blocking collectives  30 us (29%)
  starting transfers between devices  25.3 us (25%)
  Pallas kernels  24.6 us (24%)
  waiting for transfers between devices  19.2 us (19%)
  local copies, waits for them, and re-layouts  1.27 us (1%)
    all_to_all x3, starting transfers between devices, exchange(): lax.all_to_all(x, 'rows', split_axis=0, concat_axis=0, tiled=True, **more)  25.3 us
    all_to_all x3, waiting for transfers between devices, exchange(): lax.all_to_all(x, 'rows', split_axis=0, concat_axis=0, tiled=True, **more)  19.2 us
    all_to_all x1, blocking collectives, local(): lax.all_to_all(share, 'feat', split_axis=0, concat_axis=0, tiled=True)  18 us
    all_to_all x1, blocking collectives, exchange(): lax.all_to_all(x, 'rows', split_axis=0, concat_axis=0, tiled=True, **more)  12 us
    pallas_call x1, Pallas kernels, local(): call(histogram_kernel, [SMEM] + [VMEM] * 3, [((4, SPAN, BINS), F32), ((2,...  9.15 us
    pallas_call x1, Pallas kernels, local(): call(sort_kernel, [SMEM] * 3 + [VMEM] * 4, [((PEERS, CHUNK, 128), BF16),...  5.88 us
    pallas_call x1, Pallas kernels, local(): call(owner_kernel, [SMEM, VMEM], [((ROWS, 2, DOC), F32)])  2.94 us
    pallas_call x1, Pallas kernels, local(): call(pick_kernel, [VMEM] * 3, [((FEATS, SHARE, 128), BF16)], [pltpu.VMEM(...  2.54 us
  transfers between devices with their start and end apart: 3, of which 3 were waited for; matrix products, arithmetic and copies ran while one was open for 0% of the time, Pallas kernels for 11%

profile of v1, /device:TPU:1, one launch (start us, length us, event | category | flops | bytes accessed | tf_op | source)
XLA Modules:
  0.0 101.7 jit_solution(12525595596241175823)
XLA Ops:
  0.6 1.8 %shard_map.113 = f32[64,1,128]{2,1,0:T(1,128)} custom-call(f32[1,256]{1,0:T(1,128)} %bitcast.19, f32[1,256]{1,0:T(1,128)} %bitcast.20, s32[1,256]{1,0:T(1,128)} %bitcast.21, s32[1,256]{1,0:T(1,128)} %bitcast.15, s32[1,256]{1,0:T(1,128)} %bitcast.17), custom_call_target="tpu_custom_call" | custom-call | tf_op jit(solution)/shard_map/pallas_call | solution.py:335
  2.5 11.6 %all-to-all-start = ((f32[64,1,128]{2,1,0:T(1,128)}), f32[64,1,128]{2,1,0:T(1,128)S(1)}, u32[]{:S(2)}, u32[]{:S(2)}) async-start(f32[64,1,128]{2,1,0:T(1,128)} %shard_map.113), calls=%async_computation | async-start | bytes 65536 | tf_op jit(solution)/shard_map/all_to_all | solution.py:322
  14.1 5.9 %shard_map.115 = (bf16[16,88,128]{2,1,0:T(8,128)(2,1)}, f32[1,2048]{1,0:T(1,128)}) custom-call(s32[16]{0:T(128)} %feat_ref.1, s32[16]{0:T(128)} %thr_ref.1, s32[1]{0:T(128)} %bitcast.col_ref, s32[1,2048]{1,0:T(1,128)} %bitcast.12, s32[64,2048]{1,0:T(8,128)} %bins_ref.1, s32[1,256]{1,0:T(1,128)} %bitcast.16, s32[1,256]{1,0:T(1,128)} %bitcast.18), custom_call_target="tpu_custom_call" | custom-call | tf_op jit(solution)/shard_map/pallas_call | solution.py:339
  20.0 3.4 %all-to-all-done.in_ref = f32[64,1,128]{2,1,0:T(1,128)S(1)} async-done(((f32[64,1,128]{2,1,0:T(1,128)}), f32[64,1,128]{2,1,0:T(1,128)S(1)}, u32[]{:S(2)}, u32[]{:S(2)}) %all-to-all-start) | async-done | bytes 32800 | tf_op jit(solution)/shard_map/all_to_all | solution.py:322
  23.3 0.0 copy-start.2
  23.3 0.6 copy-done.2
  23.9 4.2 %all-to-all-start.2 = ((bf16[16,88,128]{2,1,0:T(8,128)(2,1)}), bf16[16,88,128]{2,1,0:T(8,128)(2,1)S(1)}, u32[]{:S(2)}, u32[]{:S(2)}) async-start(bf16[16,88,128]{2,1,0:T(8,128)(2,1)} %get-tuple-element.8), calls=%async_computation.2 | async-start | bytes 720896 | tf_op jit(solution)/shard_map/all_to_all | solution.py:322
  28.2 2.9 %shard_map.114 = f32[64,2,256]{2,1,0:T(2,128)} custom-call(s32[1,4]{1,0:T(1,128)} %len_ref.1, f32[64,1,128]{2,1,0:T(1,128)} %copy-done.2), custom_call_target="tpu_custom_call" | custom-call | tf_op jit(solution)/shard_map/pallas_call | solution.py:354
  31.1 7.8 %all-to-all-done.2.in_ref = bf16[16,88,128]{2,1,0:T(8,128)(2,1)S(1)} async-done(((bf16[16,88,128]{2,1,0:T(8,128)(2,1)}), bf16[16,88,128]{2,1,0:T(8,128)(2,1)S(1)}, u32[]{:S(2)}, u32[]{:S(2)}) %all-to-all-start.2) | async-done | bytes 360480 | tf_op jit(solution)/shard_map/all_to_all | solution.py:322
  38.9 0.0 copy-start
  38.9 9.5 %all-to-all-start.1 = ((f32[64,2,256]{2,1,0:T(2,128)}), f32[64,2,256]{2,1,0:T(2,128)S(1)}, u32[]{:S(2)}, u32[]{:S(2)}) async-start(f32[64,2,256]{2,1,0:T(2,128)} %shard_map.114), calls=%async_computation.1 | async-start | bytes 262144 | tf_op jit(solution)/shard_map/all_to_all | solution.py:322
  48.4 0.0 copy-done
  48.4 2.3 %shard_map.116 = (bf16[64,2560]{1,0:T(8,128)(2,1)}, f32[3,4,8,128]{3,2,1,0:T(8,128)}) custom-call(bf16[16,88,128]{2,1,0:T(8,128)(2,1)} %copy-done), custom_call_target="tpu_custom_call" | custom-call | tf_op jit(solution)/shard_map/pallas_call | solution.py:356
  50.7 8.0 %all-to-all-done.1.grads_ref = f32[64,2,256]{2,1,0:T(2,128)S(1)} async-done(((f32[64,2,256]{2,1,0:T(2,128)}), f32[64,2,256]{2,1,0:T(2,128)S(1)}, u32[]{:S(2)}, u32[]{:S(2)}) %all-to-all-start.1) | async-done | bytes 131104 | tf_op jit(solution)/shard_map/all_to_all | solution.py:322
  58.8 0.0 copy-start.1
  58.8 0.7 copy-done.1
  59.4 2.5 %shard_map.117 = bf16[8,64,128]{2,1,0:T(8,128)(2,1)} custom-call(f32[64,2,256]{2,1,0:T(2,128)} %copy-done.1, f32[3,4,8,128]{3,2,1,0:T(8,128)} %get-tuple-element.9.extra_ref, f32[16,128]{1,0:T(8,128)} %bitcast.14), custom_call_target="tpu_custom_call" | custom-call | tf_op jit(solution)/shard_map/pallas_call | solution.py:359
  62.0 18.0 %all_to_all.25.shares_ref = bf16[8,64,128]{2,1,0:T(8,128)(2,1)} all-to-all(bf16[8,64,128]{2,1,0:T(8,128)(2,1)} %shard_map.117), channel_id=1, replica_groups=mesh['rows'=64,'feat'=8] {'feat'}, dimensions={0} | all-to-all | bytes 262144 | tf_op jit(solution)/shard_map/all_to_all | solution.py:362
  79.9 9.1 %shard_map.118 = (f32[4,64,256]{2,1,0:T(8,128)}, s32[2,128]{1,0:T(2,128)}) custom-call(s32[1]{0:T(128)} %bitcast.col_ref, bf16[8,64,128]{2,1,0:T(8,128)(2,1)} %all_to_all.25.shares_ref, bf16[64,2560]{1,0:T(8,128)(2,1)} %get-tuple-element.11.bins_ref, s32[16,128]{1,0:T(8,128)} %bitcast.13), custom_call_target="tpu_custom_call" | custom-call | tf_op jit(solution)/shard_map/pallas_call | solution.py:363
  89.1 12.0 %all_to_all.26 = f32[4,64,256]{2,1,0:T(8,128)S(1)} all-to-all(f32[4,64,256]{2,1,0:T(8,128)} %get-tuple-element.12), channel_id=1, replica_groups={{0,8,256,264},{16,24,272,280},{32,40,288,296},{48,56,304,312},{64,72,32..., dimensions={0} | all-to-all | bytes 524288 | tf_op jit(solution)/shard_map/all_to_all | solution.py:322
  101.1 0.6 reduce_sum.9
Async XLA Ops:
  2.5 20.9 %all-to-all-start = ((f32[64,1,128]{2,1,0:T(1,128)}), f32[64,1,128]{2,1,0:T(1,128)S(1)}, u32[]{:S(2)}, u32[]{:S(2)}) async-start(f32[64,1,128]{2,1,0:T(1,128)} %shard_map.113), calls=%async_computation | async-start | bytes 65536 | tf_op jit(solution)/shard_map/all_to_all | solution.py:322
  23.3 0.6 copy-start.2
  23.9 15.0 %all-to-all-start.2 = ((bf16[16,88,128]{2,1,0:T(8,128)(2,1)}), bf16[16,88,128]{2,1,0:T(8,128)(2,1)S(1)}, u32[]{:S(2)}, u32[]{:S(2)}) async-start(bf16[16,88,128]{2,1,0:T(8,128)(2,1)} %get-tuple-element.8), calls=%async_computation.2 | async-start | bytes 720896 | tf_op jit(solution)/shard_map/all_to_all | solution.py:322
  38.9 9.5 %copy-start = (bf16[16,88,128]{2,1,0:T(8,128)(2,1)}, bf16[16,88,128]{2,1,0:T(8,128)(2,1)S(1)}, u32[]{:S(2)}) copy-start(bf16[16,88,128]{2,1,0:T(8,128)(2,1)S(1)} %all-to-all-done.2.in_ref) | copy-start | bytes 1081348
  38.9 19.8 %all-to-all-start.1 = ((f32[64,2,256]{2,1,0:T(2,128)}), f32[64,2,256]{2,1,0:T(2,128)S(1)}, u32[]{:S(2)}, u32[]{:S(2)}) async-start(f32[64,2,256]{2,1,0:T(2,128)} %shard_map.114), calls=%async_computation.1 | async-start | bytes 262144 | tf_op jit(solution)/shard_map/all_to_all | solution.py:322
  58.8 0.7 copy-start.1

commit v2 on v1

--- a/solution.py
+++ b/solution.py
@@ -156,14 +156,13 @@
     scale = w_j * inverse
     grad = jnp.sum(push, axis=0, keepdims=True) * scale
     hess = jnp.sum(bend, axis=0, keepdims=True) * scale
-    grad = grad.astype(BF16).astype(F32)
-    hess = hess.astype(BF16).astype(F32)
-    both = jnp.concatenate([grad, hess], axis=0)
-    out_ref[...] = jnp.broadcast_to(both.reshape(1, 2, DOC), (ROWS, 2, DOC))
+    both = jnp.concatenate([grad, hess], axis=0).astype(BF16)
+    for r in range(ROWS):
+        out_ref[r] = both
 
 
 def sort_kernel(
-    feat_ref, thr_ref, col_ref, parent_ref, bins_ref, owner_ref, slot_ref, out_ref, bits_ref, fold_ref, left_ref
+    feat_ref, thr_ref, col_ref, parent_ref, bins_ref, owner_ref, slot_ref, out_ref, bits_ref, fold_ref, left_ref, tail_ref
 ):
     column = col_ref[0]
     parent = parent_ref[...]
@@ -177,7 +176,7 @@
         before = nn(hot_b[:, block * DOC : (block + 1) * DOC], earlier) + carry
         ranks.append(jnp.sum(part * before, axis=0, keepdims=True))
         carry = carry + jnp.sum(part, axis=1, keepdims=True)
-    target = parent.astype(F32) * float(CAP) + jnp.concatenate(ranks, axis=1)
+    rank = jnp.concatenate(ranks, axis=1)
 
     bits = jnp.zeros((1, GROUP), F32)
     for p in range(PARENTS):
@@ -192,32 +191,36 @@
     owner = jnp.concatenate([owner_ref[...].astype(F32) + 1.0] * FEATS, axis=1)
     slot = jnp.concatenate([slot_ref[...].astype(F32)] * FEATS, axis=1)
     left_ref[0:SPAN, :] = bins_ref[...].astype(F32).astype(BF16)
-    extra = [jnp.where(own, owner, 0.0), jnp.where(own, slot, 0.0), bits, jnp.zeros_like(bits)]
-    for q in range(4):
-        left_ref[SPAN + q * 16 : SPAN + q * 16 + 16, :] = jnp.broadcast_to(extra[q], (16, GROUP)).astype(BF16)
+    extra = [jnp.where(own, owner, 0.0), jnp.where(own, slot, 0.0), bits]
+    left_ref[SPAN : SPAN + 16, :] = stack_rows(extra, 16, GROUP).astype(BF16)
 
     left = left_ref[...]
-    line = iota((256, GROUP), 0).astype(F32)
-    for pair in range(SLOTS // 256):
-        pick = as_hot(line == (target - float(256 * pair)))
-        got = nt(left, pick).astype(BF16)
-        for half in range(2):
-            t = pair * 2 + half
-            for q in range(4):
-                lanes = slice(q * 128, q * 128 + 128)
-                cols = slice(half * 128, half * 128 + 128)
-                fold_ref[t * 16 : t * 16 + 16, lanes] = got[q * 16 : q * 16 + 16, cols]
-                fold_ref[320 + t * 16 : 336 + t * 16, lanes] = got[64 + q * 16 : 80 + q * 16, cols]
+    pick = as_hot(iota((CAP, GROUP), 0).astype(F32) == rank)
+    each = jnp.concatenate([left * hot_b[p : p + 1, :] for p in range(PARENTS)], axis=0)
+    gathered = nt(each, pick)
+    for p in range(PARENTS):
+        got = gathered[p * 80 : p * 80 + 80, :]
+        low = got.astype(BF16)
+        for q in range(4):
+            lanes = slice(q * 128, q * 128 + 128)
+            rows = slice(q * 16, q * 16 + 16)
+            fold_ref[p * 16 : p * 16 + 16, lanes] = low[rows, 0:128]
+            ext = jnp.broadcast_to(got[SPAN + q : SPAN + q + 1, :], (16, CAP)).astype(BF16)
+            fold_ref[256 + p * 16 : 272 + p * 16, lanes] = ext[:, 0:128]
+            tail_ref[p * 16 : p * 16 + 16, q * 32 : q * 32 + 32] = low[rows, 128:160]
+            tail_ref[256 + p * 16 : 272 + p * 16, q * 32 : q * 32 + 32] = ext[:, 128:160]
     folded = nn(fold_ref[...], swap_matrix())
     which = iota((16, 128), 0)
     for p in range(PARENTS):
-        tail = jnp.zeros((16, 128), F32)
-        for g in range(5):
-            t, a = divmod(p * 5 + g, 4)
-            block = folded[t * 16 : t * 16 + 16, a * 128 : a * 128 + 128].astype(BF16)
-            out_ref[p, g * 16 : g * 16 + 16, :] = block
-            tail = jnp.where(which == g, folded[320 + t * 16 : 336 + t * 16, a * 128 : a * 128 + 128], tail)
-        out_ref[p, 80:88, :] = tail[0:8].astype(BF16)
+        for g in range(4):
+            out_ref[p, g * 16 : g * 16 + 16, :] = folded[
+                p * 16 : p * 16 + 16, g * 128 : g * 128 + 128
+            ].astype(BF16)
+        out_ref[p, 64:80, :] = tail_ref[p * 16 : p * 16 + 16, :]
+        last = tail_ref[256 + p * 16 : 272 + p * 16, :].astype(F32)
+        for g in range(4):
+            last = jnp.where(which == g, folded[256 + p * 16 : 272 + p * 16, g * 128 : g * 128 + 128], last)
+        out_ref[p, 80:88, :] = last[0:8].astype(BF16)
 
 
 def open_kernel(in_ref, bins_ref, extra_ref):
@@ -236,7 +239,7 @@
 
 
 def pick_kernel(grads_ref, extra_ref, bits_ref, out_ref, all_ref):
-    turned = jnp.concatenate([jnp.transpose(grads_ref[:, k, :]) for k in range(2)], axis=0)
+    turned = jnp.concatenate([jnp.transpose(grads_ref[:, k, :].astype(F32)) for k in range(2)], axis=0)
     turned = turned.astype(BF16)
     owner_line = (iota((ROWS, 128), 0) + 1).astype(F32)
     slot_line = iota((DOC, 128), 0).astype(F32)
@@ -256,7 +259,7 @@
         out_ref[c] = all_ref[...].astype(BF16)
 
 
-def histogram_kernel(col_ref, shares_ref, bins_ref, parent_ref, out_ref, node_ref, sums_ref, vals_ref):
+def histogram_kernel(col_ref, shares_ref, bins_ref, parent_ref, out_ref, node_ref, sums_ref, vals_ref, acc_ref):
     sums = shares_ref[0].astype(F32)
     for c in range(1, FEATS):
         sums = sums + shares_ref[c].astype(F32)
@@ -293,9 +296,13 @@
             hit = high == jnp.array(h, BF16)
             tall += [jnp.where(hit, v, zero) for v in vals]
         flat = [jnp.where(low == jnp.array(2 * l, BF16), one, zero) for l in range(16)]
-        acc = nt(jnp.concatenate(tall, axis=0), jnp.concatenate(flat, axis=0))
-        parts = three_parts(jnp.where(own, acc, 0.0))
-        wide = sum([nn(part.astype(BF16), fold) for part in parts])
+        acc_ref[g * 256 : g * 256 + 256, :] = nt(jnp.concatenate(tall, axis=0), jnp.concatenate(flat, axis=0))
+    two = jnp.concatenate([fold, fold], axis=0)
+    for g in range(SPAN // 8):
+        acc = jnp.where(own, acc_ref[g * 256 : g * 256 + 256, :], 0.0)
+        top = acc.astype(BF16)
+        rest = (acc - top.astype(F32)).astype(BF16)
+        wide = nn(jnp.concatenate([top, rest], axis=1), two)
         total = jnp.zeros((32, 256), F32)
         for h in range(8):
             total = jnp.where(block == h, wide[h * 32 : h * 32 + 32, :], total)
@@ -310,12 +317,16 @@
 def call(kernel, ins, outs, scratch=(), **more):
     return pl.pallas_call(
         kernel,
-        out_shape=[jax.ShapeDtypeStruct(s, d) for s, d in outs],
+        out_shape=[pltpu.VMEM(s, d) for s, d in outs],
         in_specs=list(ins),
         out_specs=[VMEM] * len(outs),
         scratch_shapes=list(scratch),
         **more,
     )
+
+
+def near(x):
+    return pltpu.with_memory_space_constraint(x, pltpu.VMEM)
 
 
 def exchange(x, **more):
@@ -340,7 +351,7 @@
         sort_kernel,
         [SMEM] * 3 + [VMEM] * 4,
         [((PEERS, CHUNK, 128), BF16), ((1, GROUP), F32)],
-        [pltpu.VMEM((640, 512), BF16), pltpu.VMEM((128, GROUP), BF16)],
+        [pltpu.VMEM((512, 512), BF16), pltpu.VMEM((80, GROUP), BF16), pltpu.VMEM((512, 128), BF16)],
     )(
         split_feat,
         split_thr,
@@ -351,21 +362,25 @@
         line(owner_slot),
     )
     taken = exchange(sorted_docs, axis_index_groups=classes)
-    (spread,) = call(owner_kernel, [SMEM, VMEM], [((ROWS, 2, DOC), F32)])(query_len, inbound)
+    (spread,) = call(owner_kernel, [SMEM, VMEM], [((ROWS, 2, DOC), BF16)])(query_len, near(inbound))
     grads = exchange(spread)
     bins, extra = call(
         open_kernel, [VMEM], [((SPAN, TAKEN), BF16), ((3, PEERS // 4, 8, 128), F32)]
-    )(taken)
+    )(near(taken))
     (share,) = call(
         pick_kernel, [VMEM] * 3, [((FEATS, SHARE, 128), BF16)], [pltpu.VMEM((SHARE, 128), F32)]
-    )(grads, extra, bits.reshape(16, 128))
+    )(near(grads), near(extra), near(bits.reshape(16, 128)))
     shares = lax.all_to_all(share, "feat", split_axis=0, concat_axis=0, tiled=True)
     rows, new_node = call(
         histogram_kernel,
         [SMEM] + [VMEM] * 3,
         [((4, SPAN, BINS), F32), ((2, 128), I32)],
-        [pltpu.VMEM((SHARE, 128), F32), pltpu.VMEM((32, TAKEN), BF16)],
-    )(column, shares, bins, parent.reshape(16, 128))
+        [
+            pltpu.VMEM((SHARE, 128), F32),
+            pltpu.VMEM((32, TAKEN), BF16),
+            pltpu.VMEM((SPAN // 8 * 256, 256), F32),
+        ],
+    )(column, near(shares), near(bins), parent.reshape(16, 128))
     came = exchange(rows, axis_index_groups=quads)
     return (jnp.sum(came, axis=0, keepdims=True), new_node.reshape(DOC))
 

time: 102 us -> 93 us (0.912)
  blocking collectives: 30 us -> 17.7 us
  Pallas kernels: 24.6 us -> 15.6 us
  waiting for transfers between devices: 19.2 us -> 27.7 us
  starting transfers between devices: 25.3 us -> 29.6 us
    all_to_all x1 -> x0, blocking collectives: 12 us -> none  [exchange(): lax.all_to_all(x, 'rows', split_axis=0, concat_axis=0, tiled=True, **more)]
    all_to_all x3 -> x4, waiting for transfers between devices: 19.2 us -> 27.7 us  [exchange(): lax.all_to_all(x, 'rows', split_axis=0, concat_axis=0, tiled=True, **more)]
    all_to_all x3 -> x4, starting transfers between devices: 25.3 us -> 29.6 us  [exchange(): lax.all_to_all(x, 'rows', split_axis=0, concat_axis=0, tiled=True, **more)]
    pallas_call x1, Pallas kernels: 9.15 us -> 4.92 us  [local(): call(histogram_kernel, [SMEM] + [VMEM] * 3, [((4, SPAN, BINS), F32), ((2,...]
    pallas_call x1, Pallas kernels: 2.29 us -> 0.58 us  [local(): call(open_kernel, [VMEM], [((SPAN, TAKEN), BF16), ((3, PEERS // 4, 8, 128...]
    pallas_call x1, Pallas kernels: 2.54 us -> 0.97 us  [local(): call(pick_kernel, [VMEM] * 3, [((FEATS, SHARE, 128), BF16)], [pltpu.VMEM(...]
    pallas_call x1, Pallas kernels: 5.88 us -> 4.47 us  [local(): call(sort_kernel, [SMEM] * 3 + [VMEM] * 4, [((PEERS, CHUNK, 128), BF16),...]
  transfers between devices with their start and end apart: 3 -> 4, of which waited for: 3 -> 4; matrix products, arithmetic and copies ran while one was open for 0% -> 1% of each run, Pallas kernels for 11% -> 9%
where the time goes in v2:
time: 93 us; the launch traced here: 92.5 us
  starting transfers between devices  29.6 us (32%)
  waiting for transfers between devices  27.7 us (30%)
  blocking collectives  17.7 us (19%)
  Pallas kernels  15.6 us (17%)
    all_to_all x4, starting transfers between devices, exchange(): lax.all_to_all(x, 'rows', split_axis=0, concat_axis=0, tiled=True, **more)  29.6 us
    all_to_all x4, waiting for transfers between devices, exchange(): lax.all_to_all(x, 'rows', split_axis=0, concat_axis=0, tiled=True, **more)  27.7 us
    all_to_all x1, blocking collectives, local(): lax.all_to_all(share, 'feat', split_axis=0, concat_axis=0, tiled=True)  17.7 us
    pallas_call x1, Pallas kernels, local(): call(histogram_kernel, [SMEM] + [VMEM] * 3, [((4, SPAN, BINS), F32), ((2,...  4.92 us
    pallas_call x1, Pallas kernels, local(): call(sort_kernel, [SMEM] * 3 + [VMEM] * 4, [((PEERS, CHUNK, 128), BF16),...  4.47 us
    pallas_call x1, Pallas kernels, local(): call(owner_kernel, [SMEM, VMEM], [((ROWS, 2, DOC), BF16)])  2.83 us
  transfers between devices with their start and end apart: 4, of which 4 were waited for; matrix products, arithmetic and copies ran while one was open for 1% of the time, Pallas kernels for 9%

profile of v2, /device:TPU:1, one launch (start us, length us, event | category | flops | bytes accessed | tf_op | source)
XLA Modules:
  0.0 92.5 jit_solution(3170970204923224433)
XLA Ops:
  0.6 1.8 %shard_map.113 = f32[64,1,128]{2,1,0:T(1,128)} custom-call(f32[1,256]{1,0:T(1,128)} %bitcast.20, f32[1,256]{1,0:T(1,128)} %bitcast.21, s32[1,256]{1,0:T(1,128)} %bitcast.22, s32[1,256]{1,0:T(1,128)} %bitcast.16, s32[1,256]{1,0:T(1,128)} %bitcast.18), custom_call_target="tpu_custom_call" | custom-call | tf_op jit(solution)/shard_map/pallas_call | solution.py:346
  2.5 11.6 %all-to-all-start = ((f32[64,1,128]{2,1,0:T(1,128)}), f32[64,1,128]{2,1,0:T(1,128)S(1)}, u32[]{:S(2)}, u32[]{:S(2)}) async-start(f32[64,1,128]{2,1,0:T(1,128)} %shard_map.113), calls=%async_computation | async-start | bytes 65536 | tf_op jit(solution)/shard_map/all_to_all | solution.py:333
  14.1 4.5 %shard_map.115 = (bf16[16,88,128]{2,1,0:T(8,128)(2,1)}, f32[1,2048]{1,0:T(1,128)S(1)}) custom-call(s32[16]{0:T(128)} %feat_ref.1, s32[16]{0:T(128)} %thr_ref.1, s32[1]{0:T(128)} %bitcast.col_ref, s32[1,2048]{1,0:T(1,128)} %bitcast.14, s32[64,2048]{1,0:T(8,128)} %bins_ref.1, s32[1,256]{1,0:T(1,128)} %bitcast.17, s32[1,256]{1,0:T(1,128)} %bitcast.19), custom_call_target="tpu_custom_call" | custom-call | tf_op jit(solution)/shard_map/pallas_call | solution.py:350
  18.6 4.8 %all-to-all-done.in_ref = f32[64,1,128]{2,1,0:T(1,128)S(1)} async-done(((f32[64,1,128]{2,1,0:T(1,128)}), f32[64,1,128]{2,1,0:T(1,128)S(1)}, u32[]{:S(2)}, u32[]{:S(2)}) %all-to-all-start) | async-done | bytes 32800 | tf_op jit(solution)/shard_map/all_to_all | solution.py:333
  23.3 3.5 %all-to-all-start.2 = ((bf16[16,88,128]{2,1,0:T(8,128)(2,1)}), bf16[16,88,128]{2,1,0:T(8,128)(2,1)S(1)}, u32[]{:S(2)}, u32[]{:S(2)}) async-start(bf16[16,88,128]{2,1,0:T(8,128)(2,1)} %get-tuple-element.8), calls=%async_computation.2 | async-start | bytes 720896 | tf_op jit(solution)/shard_map/all_to_all | solution.py:333
  26.9 2.8 %shard_map.114 = bf16[64,2,256]{2,1,0:T(2,128)(2,1)} custom-call(s32[1,4]{1,0:T(1,128)} %len_ref.1, f32[64,1,128]{2,1,0:T(1,128)S(1)} %all-to-all-done.in_ref), custom_call_target="tpu_custom_call" | custom-call | tf_op jit(solution)/shard_map/pallas_call | solution.py:365
  29.7 7.8 %all-to-all-done.2.in_ref = bf16[16,88,128]{2,1,0:T(8,128)(2,1)S(1)} async-done(((bf16[16,88,128]{2,1,0:T(8,128)(2,1)}), bf16[16,88,128]{2,1,0:T(8,128)(2,1)S(1)}, u32[]{:S(2)}, u32[]{:S(2)}) %all-to-all-start.2) | async-done | bytes 360480 | tf_op jit(solution)/shard_map/all_to_all | solution.py:333
  37.5 8.9 %all-to-all-start.1 = ((bf16[64,2,256]{2,1,0:T(2,128)(2,1)}), bf16[64,2,256]{2,1,0:T(2,128)(2,1)S(1)}, u32[]{:S(2)}, u32[]{:S(2)}) async-start(bf16[64,2,256]{2,1,0:T(2,128)(2,1)} %shard_map.114), calls=%async_computation.1 | async-start | bytes 131072 | tf_op jit(solution)/shard_map/all_to_all | solution.py:333
  46.4 0.6 shard_map.116
  47.0 9.2 %all-to-all-done.1.grads_ref = bf16[64,2,256]{2,1,0:T(2,128)(2,1)S(1)} async-done(((bf16[64,2,256]{2,1,0:T(2,128)(2,1)}), bf16[64,2,256]{2,1,0:T(2,128)(2,1)S(1)}, u32[]{:S(2)}, u32[]{:S(2)}) %all-to-all-start.1) | async-done | bytes 65568 | tf_op jit(solution)/shard_map/all_to_all | solution.py:333
  56.2 1.0 %shard_map.117 = bf16[8,64,128]{2,1,0:T(8,128)(2,1)S(1)} custom-call(bf16[64,2,256]{2,1,0:T(2,128)(2,1)S(1)} %all-to-all-done.1.grads_ref, f32[3,4,8,128]{3,2,1,0:T(8,128)S(1)} %get-tuple-element.9.extra_ref, f32[16,128]{1,0:T(8,128)S(1)} %bitcast.12), custom_call_target="tpu_custom_call" | custom-call | tf_op jit(solution)/shard_map/pallas_call | solution.py:370
  57.1 17.7 %all_to_all.25.shares_ref = bf16[8,64,128]{2,1,0:T(8,128)(2,1)S(1)} all-to-all(bf16[8,64,128]{2,1,0:T(8,128)(2,1)S(1)} %shard_map.117), channel_id=1, replica_groups=mesh['rows'=64,'feat'=8] {'feat'}, dimensions={0} | all-to-all | bytes 262144 | tf_op jit(solution)/shard_map/all_to_all | solution.py:373
  74.8 4.9 %shard_map.118 = (f32[4,64,256]{2,1,0:T(8,128)}, s32[2,128]{1,0:T(2,128)S(1)}) custom-call(s32[1]{0:T(128)} %bitcast.col_ref, bf16[8,64,128]{2,1,0:T(8,128)(2,1)S(1)} %all_to_all.25.shares_ref, bf16[64,2560]{1,0:T(8,128)(2,1)S(1)} %get-tuple-element.11.bins_ref, s32[16,128]{1,0:T(8,128)} %bitcast.15), custom_call_target="tpu_custom_call" | custom-call | tf_op jit(solution)/shard_map/pallas_call | solution.py:374
  79.8 5.5 %all-to-all-start.4 = ((f32[4,64,256]{2,1,0:T(8,128)}), f32[4,64,256]{2,1,0:T(8,128)S(1)}, u32[]{:S(2)}, u32[]{:S(2)}) async-start(f32[4,64,256]{2,1,0:T(8,128)} %get-tuple-element.12), calls=%async_computation.4 | async-start | bytes 524288 | tf_op jit(solution)/shard_map/all_to_all | solution.py:333
  85.3 0.6 copy.12
  85.8 6.0 %all-to-all-done.4 = f32[4,64,256]{2,1,0:T(8,128)S(1)} async-done(((f32[4,64,256]{2,1,0:T(8,128)}), f32[4,64,256]{2,1,0:T(8,128)S(1)}, u32[]{:S(2)}, u32[]{:S(2)}) %all-to-all-start.4) | async-done | bytes 262176 | tf_op jit(solution)/shard_map/all_to_all | solution.py:333
  91.8 0.6 reduce_sum.9
Async XLA Ops:
  2.5 20.9 %all-to-all-start = ((f32[64,1,128]{2,1,0:T(1,128)}), f32[64,1,128]{2,1,0:T(1,128)S(1)}, u32[]{:S(2)}, u32[]{:S(2)}) async-start(f32[64,1,128]{2,1,0:T(1,128)} %shard_map.113), calls=%async_computation | async-start | bytes 65536 | tf_op jit(solution)/shard_map/all_to_all | solution.py:333
  23.3 14.2 %all-to-all-start.2 = ((bf16[16,88,128]{2,1,0:T(8,128)(2,1)}), bf16[16,88,128]{2,1,0:T(8,128)(2,1)S(1)}, u32[]{:S(2)}, u32[]{:S(2)}) async-start(bf16[16,88,128]{2,1,0:T(8,128)(2,1)} %get-tuple-element.8), calls=%async_computation.2 | async-start | bytes 720896 | tf_op jit(solution)/shard_map/all_to_all | solution.py:333
  37.5 18.7 %all-to-all-start.1 = ((bf16[64,2,256]{2,1,0:T(2,128)(2,1)}), bf16[64,2,256]{2,1,0:T(2,128)(2,1)S(1)}, u32[]{:S(2)}, u32[]{:S(2)}) async-start(bf16[64,2,256]{2,1,0:T(2,128)(2,1)} %shard_map.114), calls=%async_computation.1 | async-start | bytes 131072 | tf_op jit(solution)/shard_map/all_to_all | solution.py:333
  79.8 12.1 %all-to-all-start.4 = ((f32[4,64,256]{2,1,0:T(8,128)}), f32[4,64,256]{2,1,0:T(8,128)S(1)}, u32[]{:S(2)}, u32[]{:S(2)}) async-start(f32[4,64,256]{2,1,0:T(8,128)} %get-tuple-element.12), calls=%async_computation.4 | async-start | bytes 524288 | tf_op jit(solution)/shard_map/all_to_all | solution.py:333

commit v3 on v2

--- a/solution.py
+++ b/solution.py
@@ -25,6 +25,8 @@
 CHUNK = 88
 SHARE = 64
 
+SCORE_UP = 2.0**40
+
 F32 = jnp.float32
 BF16 = jnp.bfloat16
 I32 = jnp.int32
@@ -77,7 +79,7 @@
     before = nn(hot.astype(BF16), earlier_matrix())
     place = jnp.sum(hot * before, axis=0, keepdims=True)
     rows = [
-        *three_parts(score_ref[...]),
+        *three_parts(score_ref[...] * SCORE_UP),
         *three_parts(weight_ref[...]),
         slot_ref[...].astype(F32) + 1.0,
         label_ref[...].astype(F32),
@@ -102,10 +104,10 @@
         table += nn(turned[pos * 16 : pos * 16 + 16, :], hot)
     same = as_hot(iota((DOC, DOC), 0) == iota((DOC, DOC), 1))
     upright = nt(same, table.astype(BF16))
-    s_j = table[0:1] + table[1:2] + table[2:3]
+    s_j = (table[0:1] + table[1:2] + table[2:3]) * (1.0 / SCORE_UP)
     w_j = table[3:4] + table[4:5] + table[5:6]
     l_j = table[7:8]
-    s_i = upright[:, 0:1] + upright[:, 1:2] + upright[:, 2:3]
+    s_i = (upright[:, 0:1] + upright[:, 1:2] + upright[:, 2:3]) * (1.0 / SCORE_UP)
     w_i = upright[:, 3:4] + upright[:, 4:5] + upright[:, 5:6]
     l_i = upright[:, 7:8]
 
@@ -307,7 +309,7 @@
         for h in range(8):
             total = jnp.where(block == h, wide[h * 32 : h * 32 + 32, :], total)
         for k in range(4):
-            out_ref[k, g * 8 : g * 8 + 8, :] = total[k * 8 : k * 8 + 8, :]
+            out_ref[k, g * 8 : g * 8 + 8, :] = total[k * 8 : k * 8 + 8, :].astype(BF16)
 
 
 SMEM = pl.BlockSpec(memory_space=pltpu.SMEM)
@@ -374,7 +376,7 @@
     rows, new_node = call(
         histogram_kernel,
         [SMEM] + [VMEM] * 3,
-        [((4, SPAN, BINS), F32), ((2, 128), I32)],
+        [((4, SPAN, BINS), BF16), ((2, 128), I32)],
         [
             pltpu.VMEM((SHARE, 128), F32),
             pltpu.VMEM((32, TAKEN), BF16),
@@ -382,7 +384,7 @@
         ],
     )(column, near(shares), near(bins), parent.reshape(16, 128))
     came = exchange(rows, axis_index_groups=quads)
-    return (jnp.sum(came, axis=0, keepdims=True), new_node.reshape(DOC))
+    return (jnp.sum(came.astype(F32), axis=0, keepdims=True), new_node.reshape(DOC))
 
 
 def solution(mesh):

time: 93 us -> 91.4 us (0.983)
  waiting for transfers between devices: 27.7 us -> 26.2 us
    all_to_all x4, waiting for transfers between devices: 27.7 us -> 26.2 us  [exchange(): lax.all_to_all(x, 'rows', split_axis=0, concat_axis=0, tiled=True, **more)]
where the time goes in v3:
time: 91.4 us; the launch traced here: 90.9 us
  starting transfers between devices  29.5 us (32%)
  waiting for transfers between devices  26.2 us (29%)
  blocking collectives  17.7 us (19%)
  Pallas kernels  15.6 us (17%)
    all_to_all x4, starting transfers between devices, exchange(): lax.all_to_all(x, 'rows', split_axis=0, concat_axis=0, tiled=True, **more)  29.5 us
    all_to_all x4, waiting for transfers between devices, exchange(): lax.all_to_all(x, 'rows', split_axis=0, concat_axis=0, tiled=True, **more)  26.2 us
    all_to_all x1, blocking collectives, local(): lax.all_to_all(share, 'feat', split_axis=0, concat_axis=0, tiled=True)  17.7 us
    pallas_call x1, Pallas kernels, local(): call(histogram_kernel, [SMEM] + [VMEM] * 3, [((4, SPAN, BINS), BF16), ((2...  4.88 us
    pallas_call x1, Pallas kernels, local(): call(sort_kernel, [SMEM] * 3 + [VMEM] * 4, [((PEERS, CHUNK, 128), BF16),...  4.47 us
    pallas_call x1, Pallas kernels, local(): call(owner_kernel, [SMEM, VMEM], [((ROWS, 2, DOC), BF16)])  2.83 us
    pallas_call x1, Pallas kernels, local(): call(send_kernel, [VMEM] * 5, [((ROWS, 1, 128), F32)])  1.83 us
  transfers between devices with their start and end apart: 4, of which 4 were waited for; matrix products, arithmetic and copies ran while one was open for 1% of the time, Pallas kernels for 9%

profile of v3, /device:TPU:1, one launch (start us, length us, event | category | flops | bytes accessed | tf_op | source)
XLA Modules:
  0.0 90.9 jit_solution(5961344196663045642)
XLA Ops:
  0.6 1.8 %shard_map.113 = f32[64,1,128]{2,1,0:T(1,128)} custom-call(f32[1,256]{1,0:T(1,128)} %bitcast.20, f32[1,256]{1,0:T(1,128)} %bitcast.21, s32[1,256]{1,0:T(1,128)} %bitcast.22, s32[1,256]{1,0:T(1,128)} %bitcast.16, s32[1,256]{1,0:T(1,128)} %bitcast.18), custom_call_target="tpu_custom_call" | custom-call | tf_op jit(solution)/shard_map/pallas_call | solution.py:348
  2.5 11.6 %all-to-all-start = ((f32[64,1,128]{2,1,0:T(1,128)}), f32[64,1,128]{2,1,0:T(1,128)S(1)}, u32[]{:S(2)}, u32[]{:S(2)}) async-start(f32[64,1,128]{2,1,0:T(1,128)} %shard_map.113), calls=%async_computation | async-start | bytes 65536 | tf_op jit(solution)/shard_map/all_to_all | solution.py:335
  14.1 4.5 %shard_map.115 = (bf16[16,88,128]{2,1,0:T(8,128)(2,1)}, f32[1,2048]{1,0:T(1,128)S(1)}) custom-call(s32[16]{0:T(128)} %feat_ref.1, s32[16]{0:T(128)} %thr_ref.1, s32[1]{0:T(128)} %bitcast.col_ref, s32[1,2048]{1,0:T(1,128)} %bitcast.14, s32[64,2048]{1,0:T(8,128)} %bins_ref.1, s32[1,256]{1,0:T(1,128)} %bitcast.17, s32[1,256]{1,0:T(1,128)} %bitcast.19), custom_call_target="tpu_custom_call" | custom-call | tf_op jit(solution)/shard_map/pallas_call | solution.py:352
  18.6 4.8 %all-to-all-done.in_ref = f32[64,1,128]{2,1,0:T(1,128)S(1)} async-done(((f32[64,1,128]{2,1,0:T(1,128)}), f32[64,1,128]{2,1,0:T(1,128)S(1)}, u32[]{:S(2)}, u32[]{:S(2)}) %all-to-all-start) | async-done | bytes 32800 | tf_op jit(solution)/shard_map/all_to_all | solution.py:335
  23.3 3.5 %all-to-all-start.2 = ((bf16[16,88,128]{2,1,0:T(8,128)(2,1)}), bf16[16,88,128]{2,1,0:T(8,128)(2,1)S(1)}, u32[]{:S(2)}, u32[]{:S(2)}) async-start(bf16[16,88,128]{2,1,0:T(8,128)(2,1)} %get-tuple-element.8), calls=%async_computation.2 | async-start | bytes 720896 | tf_op jit(solution)/shard_map/all_to_all | solution.py:335
  26.9 2.8 %shard_map.114 = bf16[64,2,256]{2,1,0:T(2,128)(2,1)} custom-call(s32[1,4]{1,0:T(1,128)} %len_ref.1, f32[64,1,128]{2,1,0:T(1,128)S(1)} %all-to-all-done.in_ref), custom_call_target="tpu_custom_call" | custom-call | tf_op jit(solution)/shard_map/pallas_call | solution.py:367
  29.7 7.8 %all-to-all-done.2.in_ref = bf16[16,88,128]{2,1,0:T(8,128)(2,1)S(1)} async-done(((bf16[16,88,128]{2,1,0:T(8,128)(2,1)}), bf16[16,88,128]{2,1,0:T(8,128)(2,1)S(1)}, u32[]{:S(2)}, u32[]{:S(2)}) %all-to-all-start.2) | async-done | bytes 360480 | tf_op jit(solution)/shard_map/all_to_all | solution.py:335
  37.5 8.9 %all-to-all-start.1 = ((bf16[64,2,256]{2,1,0:T(2,128)(2,1)}), bf16[64,2,256]{2,1,0:T(2,128)(2,1)S(1)}, u32[]{:S(2)}, u32[]{:S(2)}) async-start(bf16[64,2,256]{2,1,0:T(2,128)(2,1)} %shard_map.114), calls=%async_computation.1 | async-start | bytes 131072 | tf_op jit(solution)/shard_map/all_to_all | solution.py:335
  46.4 0.6 shard_map.116
  47.0 9.2 %all-to-all-done.1.grads_ref = bf16[64,2,256]{2,1,0:T(2,128)(2,1)S(1)} async-done(((bf16[64,2,256]{2,1,0:T(2,128)(2,1)}), bf16[64,2,256]{2,1,0:T(2,128)(2,1)S(1)}, u32[]{:S(2)}, u32[]{:S(2)}) %all-to-all-start.1) | async-done | bytes 65568 | tf_op jit(solution)/shard_map/all_to_all | solution.py:335
  56.2 1.0 %shard_map.117 = bf16[8,64,128]{2,1,0:T(8,128)(2,1)S(1)} custom-call(bf16[64,2,256]{2,1,0:T(2,128)(2,1)S(1)} %all-to-all-done.1.grads_ref, f32[3,4,8,128]{3,2,1,0:T(8,128)S(1)} %get-tuple-element.9.extra_ref, f32[16,128]{1,0:T(8,128)S(1)} %bitcast.12), custom_call_target="tpu_custom_call" | custom-call | tf_op jit(solution)/shard_map/pallas_call | solution.py:372
  57.1 17.7 %all_to_all.25.shares_ref = bf16[8,64,128]{2,1,0:T(8,128)(2,1)S(1)} all-to-all(bf16[8,64,128]{2,1,0:T(8,128)(2,1)S(1)} %shard_map.117), channel_id=1, replica_groups=mesh['rows'=64,'feat'=8] {'feat'}, dimensions={0} | all-to-all | bytes 262144 | tf_op jit(solution)/shard_map/all_to_all | solution.py:375
  74.8 4.9 %shard_map.118 = (bf16[4,64,256]{2,1,0:T(8,128)(2,1)}, s32[2,128]{1,0:T(2,128)S(1)}) custom-call(s32[1]{0:T(128)} %bitcast.col_ref, bf16[8,64,128]{2,1,0:T(8,128)(2,1)S(1)} %all_to_all.25.shares_ref, bf16[64,2560]{1,0:T(8,128)(2,1)S(1)} %get-tuple-element.11.bins_ref, s32[16,128]{1,0:T(8,128)} %bitcast.15), custom_call_target="tpu_custom_call" | custom-call | tf_op jit(solution)/shard_map/pallas_call | solution.py:376
  79.7 5.4 %all-to-all-start.4 = ((bf16[4,64,256]{2,1,0:T(8,128)(2,1)}), bf16[4,64,256]{2,1,0:T(8,128)(2,1)S(1)}, u32[]{:S(2)}, u32[]{:S(2)}) async-start(bf16[4,64,256]{2,1,0:T(8,128)(2,1)} %get-tuple-element.12), calls=%async_computation.4 | async-start | bytes 262144 | tf_op jit(solution)/shard_map/all_to_all | solution.py:335
  85.2 0.6 copy.12
  85.7 4.5 %all-to-all-done.4 = bf16[4,64,256]{2,1,0:T(8,128)(2,1)S(1)} async-done(((bf16[4,64,256]{2,1,0:T(8,128)(2,1)}), bf16[4,64,256]{2,1,0:T(8,128)(2,1)S(1)}, u32[]{:S(2)}, u32[]{:S(2)}) %all-to-all-start.4) | async-done | bytes 131104 | tf_op jit(solution)/shard_map/all_to_all | solution.py:335
  90.2 0.6 convert_reduce_fusion
Async XLA Ops:
  2.5 20.9 %all-to-all-start = ((f32[64,1,128]{2,1,0:T(1,128)}), f32[64,1,128]{2,1,0:T(1,128)S(1)}, u32[]{:S(2)}, u32[]{:S(2)}) async-start(f32[64,1,128]{2,1,0:T(1,128)} %shard_map.113), calls=%async_computation | async-start | bytes 65536 | tf_op jit(solution)/shard_map/all_to_all | solution.py:335
  23.3 14.2 %all-to-all-start.2 = ((bf16[16,88,128]{2,1,0:T(8,128)(2,1)}), bf16[16,88,128]{2,1,0:T(8,128)(2,1)S(1)}, u32[]{:S(2)}, u32[]{:S(2)}) async-start(bf16[16,88,128]{2,1,0:T(8,128)(2,1)} %get-tuple-element.8), calls=%async_computation.2 | async-start | bytes 720896 | tf_op jit(solution)/shard_map/all_to_all | solution.py:335
  37.5 18.7 %all-to-all-start.1 = ((bf16[64,2,256]{2,1,0:T(2,128)(2,1)}), bf16[64,2,256]{2,1,0:T(2,128)(2,1)S(1)}, u32[]{:S(2)}, u32[]{:S(2)}) async-start(bf16[64,2,256]{2,1,0:T(2,128)(2,1)} %shard_map.114), calls=%async_computation.1 | async-start | bytes 131072 | tf_op jit(solution)/shard_map/all_to_all | solution.py:335
  79.7 10.5 %all-to-all-start.4 = ((bf16[4,64,256]{2,1,0:T(8,128)(2,1)}), bf16[4,64,256]{2,1,0:T(8,128)(2,1)S(1)}, u32[]{:S(2)}, u32[]{:S(2)}) async-start(bf16[4,64,256]{2,1,0:T(8,128)(2,1)} %get-tuple-element.12), calls=%async_computation.4 | async-start | bytes 262144 | tf_op jit(solution)/shard_map/all_to_all | solution.py:335

commit v4 on v3

--- a/solution.py
+++ b/solution.py
@@ -164,9 +164,23 @@
 
 
 def sort_kernel(
-    feat_ref, thr_ref, col_ref, parent_ref, bins_ref, owner_ref, slot_ref, out_ref, bits_ref, fold_ref, left_ref, tail_ref
+    feat_ref,
+    thr_ref,
+    col_ref,
+    parent_ref,
+    folded_ref,
+    bins_ref,
+    owner_ref,
+    slot_ref,
+    out_ref,
+    bits_ref,
+    own_ref,
+    fold_ref,
+    left_ref,
+    tail_ref,
 ):
     column = col_ref[0]
+    own_ref[...] = folded_ref[pl.ds(2 * column, 2), :]
     parent = parent_ref[...]
     hot = jnp.where(iota((PARENTS, GROUP), 0) == parent, 1.0, 0.0)
     hot_b = hot.astype(BF16)
@@ -261,12 +275,12 @@
         out_ref[c] = all_ref[...].astype(BF16)
 
 
-def histogram_kernel(col_ref, shares_ref, bins_ref, parent_ref, out_ref, node_ref, sums_ref, vals_ref, acc_ref):
+def histogram_kernel(shares_ref, bins_ref, parent_ref, out_ref, node_ref, sums_ref, vals_ref, acc_ref):
     sums = shares_ref[0].astype(F32)
     for c in range(1, FEATS):
         sums = sums + shares_ref[c].astype(F32)
     sums_ref[...] = sums
-    node_ref[...] = 2 * parent_ref[pl.ds(2 * col_ref[0], 2), :] + sums_ref[60:62, :].astype(I32)
+    node_ref[...] = 2 * parent_ref[...] + sums_ref[60:62, :].astype(I32)
 
     child = (iota((16, 128), 0) >> 3).astype(F32)
     for t in range(TILES):
@@ -349,16 +363,17 @@
         line(scores), line(weights), line(labels), line(owner_row), line(owner_slot)
     )
     inbound = exchange(outbound)
-    sorted_docs, bits = call(
+    sorted_docs, bits, own_parent = call(
         sort_kernel,
-        [SMEM] * 3 + [VMEM] * 4,
-        [((PEERS, CHUNK, 128), BF16), ((1, GROUP), F32)],
+        [SMEM] * 3 + [VMEM] * 5,
+        [((PEERS, CHUNK, 128), BF16), ((1, GROUP), F32), ((2, 128), I32)],
         [pltpu.VMEM((512, 512), BF16), pltpu.VMEM((80, GROUP), BF16), pltpu.VMEM((512, 128), BF16)],
     )(
         split_feat,
         split_thr,
         column,
         parent.reshape(1, GROUP),
+        parent.reshape(16, 128),
         bin_index,
         line(owner_row),
         line(owner_slot),
@@ -375,14 +390,14 @@
     shares = lax.all_to_all(share, "feat", split_axis=0, concat_axis=0, tiled=True)
     rows, new_node = call(
         histogram_kernel,
-        [SMEM] + [VMEM] * 3,
+        [VMEM] * 3,
         [((4, SPAN, BINS), BF16), ((2, 128), I32)],
         [
             pltpu.VMEM((SHARE, 128), F32),
             pltpu.VMEM((32, TAKEN), BF16),
             pltpu.VMEM((SPAN // 8 * 256, 256), F32),
         ],
-    )(column, near(shares), near(bins), parent.reshape(16, 128))
+    )(near(shares), near(bins), near(own_parent))
     came = exchange(rows, axis_index_groups=quads)
     return (jnp.sum(came.astype(F32), axis=0, keepdims=True), new_node.reshape(DOC))
 

time: 91.4 us -> 90.7 us (level)
  no operation moved by 1% of the time
where the time goes in v4:
time: 90.7 us; the launch traced here: 90.3 us
  starting transfers between devices  29.6 us (33%)
  waiting for transfers between devices  26.2 us (29%)
  blocking collectives  17.7 us (20%)
  Pallas kernels  14.9 us (16%)
    all_to_all x4, starting transfers between devices, exchange(): lax.all_to_all(x, 'rows', split_axis=0, concat_axis=0, tiled=True, **more)  29.6 us
    all_to_all x4, waiting for transfers between devices, exchange(): lax.all_to_all(x, 'rows', split_axis=0, concat_axis=0, tiled=True, **more)  26.2 us
    all_to_all x1, blocking collectives, local(): lax.all_to_all(share, 'feat', split_axis=0, concat_axis=0, tiled=True)  17.7 us
    pallas_call x1, Pallas kernels, local(): call(sort_kernel, [SMEM] * 3 + [VMEM] * 5, [((PEERS, CHUNK, 128), BF16),...  4.52 us
    pallas_call x1, Pallas kernels, local(): call(histogram_kernel, [VMEM] * 3, [((4, SPAN, BINS), BF16), ((2, 128), I...  4.18 us
    pallas_call x1, Pallas kernels, local(): call(owner_kernel, [SMEM, VMEM], [((ROWS, 2, DOC), BF16)])  2.83 us
    pallas_call x1, Pallas kernels, local(): call(send_kernel, [VMEM] * 5, [((ROWS, 1, 128), F32)])  1.83 us
  transfers between devices with their start and end apart: 4, of which 4 were waited for; matrix products, arithmetic and copies ran while one was open for 1% of the time, Pallas kernels for 9%

profile of v4, /device:TPU:1, one launch (start us, length us, event | category | flops | bytes accessed | tf_op | source)
XLA Modules:
  0.0 90.3 jit_solution(5661668800798153179)
XLA Ops:
  0.6 1.8 %shard_map.113 = f32[64,1,128]{2,1,0:T(1,128)} custom-call(f32[1,256]{1,0:T(1,128)} %bitcast.20, f32[1,256]{1,0:T(1,128)} %bitcast.21, s32[1,256]{1,0:T(1,128)} %bitcast.22, s32[1,256]{1,0:T(1,128)} %bitcast.16, s32[1,256]{1,0:T(1,128)} %bitcast.18), custom_call_target="tpu_custom_call" | custom-call | tf_op jit(solution)/shard_map/pallas_call | solution.py:362
  2.5 11.6 %all-to-all-start = ((f32[64,1,128]{2,1,0:T(1,128)}), f32[64,1,128]{2,1,0:T(1,128)S(1)}, u32[]{:S(2)}, u32[]{:S(2)}) async-start(f32[64,1,128]{2,1,0:T(1,128)} %shard_map.113), calls=%async_computation | async-start | bytes 65536 | tf_op jit(solution)/shard_map/all_to_all | solution.py:349
  14.1 4.5 %shard_map.115 = (bf16[16,88,128]{2,1,0:T(8,128)(2,1)}, f32[1,2048]{1,0:T(1,128)S(1)}, s32[2,128]{1,0:T(2,128)S(1)}) custom-call(s32[16]{0:T(128)} %feat_ref.1, s32[16]{0:T(128)} %thr_ref.1, s32[1]{0:T(128)} %bitcast.5.col_ref, s32[1,2048]{1,0:T(1,128)} %bitcast.14, s32[16,128]{1,0:T(8,128)} %bitcast.15, s32[64,2048]{1,0:T(8,128)} %bins_ref.1, ...), custom_call_target="tpu_custom_call" | custom-call | tf_op jit(solution)/shard_map/pallas_call | solution.py:366
  18.6 4.7 %all-to-all-done.in_ref = f32[64,1,128]{2,1,0:T(1,128)S(1)} async-done(((f32[64,1,128]{2,1,0:T(1,128)}), f32[64,1,128]{2,1,0:T(1,128)S(1)}, u32[]{:S(2)}, u32[]{:S(2)}) %all-to-all-start) | async-done | bytes 32800 | tf_op jit(solution)/shard_map/all_to_all | solution.py:349
  23.3 3.5 %all-to-all-start.2 = ((bf16[16,88,128]{2,1,0:T(8,128)(2,1)}), bf16[16,88,128]{2,1,0:T(8,128)(2,1)S(1)}, u32[]{:S(2)}, u32[]{:S(2)}) async-start(bf16[16,88,128]{2,1,0:T(8,128)(2,1)} %get-tuple-element.9), calls=%async_computation.2 | async-start | bytes 720896 | tf_op jit(solution)/shard_map/all_to_all | solution.py:349
  26.9 2.8 %shard_map.114 = bf16[64,2,256]{2,1,0:T(2,128)(2,1)} custom-call(s32[1,4]{1,0:T(1,128)} %len_ref.1, f32[64,1,128]{2,1,0:T(1,128)S(1)} %all-to-all-done.in_ref), custom_call_target="tpu_custom_call" | custom-call | tf_op jit(solution)/shard_map/pallas_call | solution.py:382
  29.7 7.8 %all-to-all-done.2.in_ref = bf16[16,88,128]{2,1,0:T(8,128)(2,1)S(1)} async-done(((bf16[16,88,128]{2,1,0:T(8,128)(2,1)}), bf16[16,88,128]{2,1,0:T(8,128)(2,1)S(1)}, u32[]{:S(2)}, u32[]{:S(2)}) %all-to-all-start.2) | async-done | bytes 360480 | tf_op jit(solution)/shard_map/all_to_all | solution.py:349
  37.5 9.0 %all-to-all-start.1 = ((bf16[64,2,256]{2,1,0:T(2,128)(2,1)}), bf16[64,2,256]{2,1,0:T(2,128)(2,1)S(1)}, u32[]{:S(2)}, u32[]{:S(2)}) async-start(bf16[64,2,256]{2,1,0:T(2,128)(2,1)} %shard_map.114), calls=%async_computation.1 | async-start | bytes 131072 | tf_op jit(solution)/shard_map/all_to_all | solution.py:349
  46.4 0.6 shard_map.116
  47.0 9.2 %all-to-all-done.1.grads_ref = bf16[64,2,256]{2,1,0:T(2,128)(2,1)S(1)} async-done(((bf16[64,2,256]{2,1,0:T(2,128)(2,1)}), bf16[64,2,256]{2,1,0:T(2,128)(2,1)S(1)}, u32[]{:S(2)}, u32[]{:S(2)}) %all-to-all-start.1) | async-done | bytes 65568 | tf_op jit(solution)/shard_map/all_to_all | solution.py:349
  56.2 1.0 %shard_map.117 = bf16[8,64,128]{2,1,0:T(8,128)(2,1)S(1)} custom-call(bf16[64,2,256]{2,1,0:T(2,128)(2,1)S(1)} %all-to-all-done.1.grads_ref, f32[3,4,8,128]{3,2,1,0:T(8,128)S(1)} %get-tuple-element.10.extra_ref, f32[16,128]{1,0:T(8,128)S(1)} %bitcast.12), custom_call_target="tpu_custom_call" | custom-call | tf_op jit(solution)/shard_map/pallas_call | solution.py:387
  57.2 17.7 %all_to_all.25.shares_ref = bf16[8,64,128]{2,1,0:T(8,128)(2,1)S(1)} all-to-all(bf16[8,64,128]{2,1,0:T(8,128)(2,1)S(1)} %shard_map.117), channel_id=1, replica_groups=mesh['rows'=64,'feat'=8] {'feat'}, dimensions={0} | all-to-all | bytes 262144 | tf_op jit(solution)/shard_map/all_to_all | solution.py:390
  74.9 4.2 %shard_map.118 = (bf16[4,64,256]{2,1,0:T(8,128)(2,1)}, s32[2,128]{1,0:T(2,128)S(1)}) custom-call(bf16[8,64,128]{2,1,0:T(8,128)(2,1)S(1)} %all_to_all.25.shares_ref, bf16[64,2560]{1,0:T(8,128)(2,1)S(1)} %get-tuple-element.12.bins_ref, s32[2,128]{1,0:T(2,128)S(1)} %get-tuple-element.13.parent_ref), custom_call_target="tpu_custom_call" | custom-call | tf_op jit(solution)/shard_map/pallas_call | solution.py:391
  79.1 5.4 %all-to-all-start.4 = ((bf16[4,64,256]{2,1,0:T(8,128)(2,1)}), bf16[4,64,256]{2,1,0:T(8,128)(2,1)S(1)}, u32[]{:S(2)}, u32[]{:S(2)}) async-start(bf16[4,64,256]{2,1,0:T(8,128)(2,1)} %get-tuple-element.14), calls=%async_computation.4 | async-start | bytes 262144 | tf_op jit(solution)/shard_map/all_to_all | solution.py:349
  84.5 0.6 copy.12
  85.1 4.5 %all-to-all-done.4 = bf16[4,64,256]{2,1,0:T(8,128)(2,1)S(1)} async-done(((bf16[4,64,256]{2,1,0:T(8,128)(2,1)}), bf16[4,64,256]{2,1,0:T(8,128)(2,1)S(1)}, u32[]{:S(2)}, u32[]{:S(2)}) %all-to-all-start.4) | async-done | bytes 131104 | tf_op jit(solution)/shard_map/all_to_all | solution.py:349
  89.6 0.6 convert_reduce_fusion
Async XLA Ops:
  2.5 20.9 %all-to-all-start = ((f32[64,1,128]{2,1,0:T(1,128)}), f32[64,1,128]{2,1,0:T(1,128)S(1)}, u32[]{:S(2)}, u32[]{:S(2)}) async-start(f32[64,1,128]{2,1,0:T(1,128)} %shard_map.113), calls=%async_computation | async-start | bytes 65536 | tf_op jit(solution)/shard_map/all_to_all | solution.py:349
  23.3 14.2 %all-to-all-start.2 = ((bf16[16,88,128]{2,1,0:T(8,128)(2,1)}), bf16[16,88,128]{2,1,0:T(8,128)(2,1)S(1)}, u32[]{:S(2)}, u32[]{:S(2)}) async-start(bf16[16,88,128]{2,1,0:T(8,128)(2,1)} %get-tuple-element.9), calls=%async_computation.2 | async-start | bytes 720896 | tf_op jit(solution)/shard_map/all_to_all | solution.py:349
  37.5 18.7 %all-to-all-start.1 = ((bf16[64,2,256]{2,1,0:T(2,128)(2,1)}), bf16[64,2,256]{2,1,0:T(2,128)(2,1)S(1)}, u32[]{:S(2)}, u32[]{:S(2)}) async-start(bf16[64,2,256]{2,1,0:T(2,128)(2,1)} %shard_map.114), calls=%async_computation.1 | async-start | bytes 131072 | tf_op jit(solution)/shard_map/all_to_all | solution.py:349
  79.1 10.5 %all-to-all-start.4 = ((bf16[4,64,256]{2,1,0:T(8,128)(2,1)}), bf16[4,64,256]{2,1,0:T(8,128)(2,1)S(1)}, u32[]{:S(2)}, u32[]{:S(2)}) async-start(bf16[4,64,256]{2,1,0:T(8,128)(2,1)} %get-tuple-element.14), calls=%async_computation.4 | async-start | bytes 262144 | tf_op jit(solution)/shard_map/all_to_all | solution.py:349

commit v5 on v4

--- a/solution.py
+++ b/solution.py
@@ -180,7 +180,8 @@
     tail_ref,
 ):
     column = col_ref[0]
-    own_ref[...] = folded_ref[pl.ds(2 * column, 2), :]
+    own = folded_ref[pl.ds(2 * column, 2), :]
+    own_ref[...] = jnp.concatenate([own[0:1], own[1:2]], axis=1)
     parent = parent_ref[...]
     hot = jnp.where(iota((PARENTS, GROUP), 0) == parent, 1.0, 0.0)
     hot_b = hot.astype(BF16)
@@ -280,7 +281,8 @@
     for c in range(1, FEATS):
         sums = sums + shares_ref[c].astype(F32)
     sums_ref[...] = sums
-    node_ref[...] = 2 * parent_ref[...] + sums_ref[60:62, :].astype(I32)
+    right = jnp.concatenate([sums_ref[60:61, :], sums_ref[61:62, :]], axis=1)
+    node_ref[...] = 2 * parent_ref[...] + right.astype(I32)
 
     child = (iota((16, 128), 0) >> 3).astype(F32)
     for t in range(TILES):
@@ -333,7 +335,7 @@
 def call(kernel, ins, outs, scratch=(), **more):
     return pl.pallas_call(
         kernel,
-        out_shape=[pltpu.VMEM(s, d) for s, d in outs],
+        out_shape=[pltpu.VMEM(*o) if len(o) == 2 else jax.ShapeDtypeStruct(*o[:2]) for o in outs],
         in_specs=list(ins),
         out_specs=[VMEM] * len(outs),
         scratch_shapes=list(scratch),
@@ -366,7 +368,7 @@
     sorted_docs, bits, own_parent = call(
         sort_kernel,
         [SMEM] * 3 + [VMEM] * 5,
-        [((PEERS, CHUNK, 128), BF16), ((1, GROUP), F32), ((2, 128), I32)],
+        [((PEERS, CHUNK, 128), BF16), ((1, GROUP), F32), ((1, DOC), I32)],
         [pltpu.VMEM((512, 512), BF16), pltpu.VMEM((80, GROUP), BF16), pltpu.VMEM((512, 128), BF16)],
     )(
         split_feat,
@@ -378,9 +380,10 @@
         line(owner_row),
         line(owner_slot),
     )
-    taken = exchange(sorted_docs, axis_index_groups=classes)
     (spread,) = call(owner_kernel, [SMEM, VMEM], [((ROWS, 2, DOC), BF16)])(query_len, near(inbound))
     grads = exchange(spread)
+    grads, sorted_docs = lax.optimization_barrier((grads, sorted_docs))
+    taken = exchange(sorted_docs, axis_index_groups=classes)
     bins, extra = call(
         open_kernel, [VMEM], [((SPAN, TAKEN), BF16), ((3, PEERS // 4, 8, 128), F32)]
     )(near(taken))
@@ -391,7 +394,7 @@
     rows, new_node = call(
         histogram_kernel,
         [VMEM] * 3,
-        [((4, SPAN, BINS), BF16), ((2, 128), I32)],
+        [((4, SPAN, BINS), BF16), ((1, DOC), I32, "hbm")],
         [
             pltpu.VMEM((SHARE, 128), F32),
             pltpu.VMEM((32, TAKEN), BF16),

time: 90.7 us -> 89 us (0.981)
  blocking collectives: 17.7 us -> 63.2 us
  starting transfers between devices: 29.6 us -> 4.71 us
  waiting for transfers between devices: 26.2 us -> 6.1 us
  Pallas kernels: 14.9 us -> 13.3 us
    all_to_all x0 -> x3, blocking collectives: none -> 45.4 us  [exchange(): lax.all_to_all(x, 'rows', split_axis=0, concat_axis=0, tiled=True, **more)]
    all_to_all x4 -> x1, starting transfers between devices: 29.6 us -> 4.71 us  [exchange(): lax.all_to_all(x, 'rows', split_axis=0, concat_axis=0, tiled=True, **more)]
    all_to_all x4 -> x1, waiting for transfers between devices: 26.2 us -> 6.1 us  [exchange(): lax.all_to_all(x, 'rows', split_axis=0, concat_axis=0, tiled=True, **more)]
  transfers between devices with their start and end apart: 4 -> 1, of which waited for: 4 -> 1; matrix products, arithmetic and copies ran while one was open for 1% -> 0% of each run, Pallas kernels for 9% -> 4%
where the time goes in v5:
time: 89 us; the launch traced here: 88.7 us
  blocking collectives  63.2 us (71%)
  Pallas kernels  13.3 us (15%)
  waiting for transfers between devices  6.1 us (7%)
  starting transfers between devices  4.71 us (5%)
    all_to_all x3, blocking collectives, exchange(): lax.all_to_all(x, 'rows', split_axis=0, concat_axis=0, tiled=True, **more)  45.4 us
    all_to_all x1, blocking collectives, local(): lax.all_to_all(share, 'feat', split_axis=0, concat_axis=0, tiled=True)  17.8 us
    all_to_all x1, waiting for transfers between devices, exchange(): lax.all_to_all(x, 'rows', split_axis=0, concat_axis=0, tiled=True, **more)  6.1 us
    all_to_all x1, starting transfers between devices, exchange(): lax.all_to_all(x, 'rows', split_axis=0, concat_axis=0, tiled=True, **more)  4.71 us
    pallas_call x1, Pallas kernels, local(): call(histogram_kernel, [VMEM] * 3, [((4, SPAN, BINS), BF16), ((1, DOC), I...  3.97 us
    pallas_call x1, Pallas kernels, local(): call(sort_kernel, [SMEM] * 3 + [VMEM] * 5, [((PEERS, CHUNK, 128), BF16),...  3.78 us
    pallas_call x1, Pallas kernels, local(): call(owner_kernel, [SMEM, VMEM], [((ROWS, 2, DOC), BF16)])  2.82 us
  transfers between devices with their start and end apart: 1, of which 1 were waited for; matrix products, arithmetic and copies ran while one was open for 0% of the time, Pallas kernels for 4%

profile of v5, /device:TPU:1, one launch (start us, length us, event | category | flops | bytes accessed | tf_op | source)
XLA Modules:
  0.0 88.7 jit_solution(12194820017854586063)
XLA Ops:
  0.6 1.2 %shard_map.113 = f32[64,1,128]{2,1,0:T(1,128)S(1)} custom-call(f32[1,256]{1,0:T(1,128)} %bitcast.19, f32[1,256]{1,0:T(1,128)} %bitcast.20, s32[1,256]{1,0:T(1,128)} %bitcast.21, s32[1,256]{1,0:T(1,128)} %bitcast.15, s32[1,256]{1,0:T(1,128)} %bitcast.17), custom_call_target="tpu_custom_call" | custom-call | tf_op jit(solution)/shard_map/pallas_call | solution.py:364
  1.9 20.7 %all_to_all.25.in_ref = f32[64,1,128]{2,1,0:T(1,128)S(1)} all-to-all(f32[64,1,128]{2,1,0:T(1,128)S(1)} %shard_map.113), channel_id=1, replica_groups=mesh['rows'=64,'feat'=8] {'rows'}, dimensions={0} | all-to-all | bytes 65536 | tf_op jit(solution)/shard_map/all_to_all | solution.py:351
  22.6 2.8 %shard_map.114 = bf16[64,2,256]{2,1,0:T(2,128)(2,1)} custom-call(s32[1,4]{1,0:T(1,128)} %len_ref.1, f32[64,1,128]{2,1,0:T(1,128)S(1)} %all_to_all.25.in_ref), custom_call_target="tpu_custom_call" | custom-call | tf_op jit(solution)/shard_map/pallas_call | solution.py:383
  25.4 4.7 %all-to-all-start.1 = ((bf16[64,2,256]{2,1,0:T(2,128)(2,1)}), bf16[64,2,256]{2,1,0:T(2,128)(2,1)S(1)}, u32[]{:S(2)}, u32[]{:S(2)}) async-start(bf16[64,2,256]{2,1,0:T(2,128)(2,1)} %shard_map.114), calls=%async_computation.1 | async-start | bytes 131072 | tf_op jit(solution)/shard_map/all_to_all | solution.py:351
  30.1 3.8 %shard_map.115 = (bf16[16,88,128]{2,1,0:T(8,128)(2,1)S(1)}, f32[1,2048]{1,0:T(1,128)S(1)}, s32[1,256]{1,0:T(1,128)S(1)}) custom-call(s32[16]{0:T(128)} %feat_ref.1, s32[16]{0:T(128)} %thr_ref.1, s32[1]{0:T(128)} %bitcast.5.col_ref, s32[1,2048]{1,0:T(1,128)} %bitcast.13, s32[16,128]{1,0:T(8,128)} %bitcast.14, s32[64,2048]{1,0:T(8,128)} %bins_ref.1, ...), custom_call_target="tpu_custom_call" | custom-call | tf_op jit(solution)/shard_map/pallas_call | solution.py:368
  33.9 6.1 %all-to-all-done.1.grads_ref = bf16[64,2,256]{2,1,0:T(2,128)(2,1)S(1)} async-done(((bf16[64,2,256]{2,1,0:T(2,128)(2,1)}), bf16[64,2,256]{2,1,0:T(2,128)(2,1)S(1)}, u32[]{:S(2)}, u32[]{:S(2)}) %all-to-all-start.1) | async-done | bytes 65568 | tf_op jit(solution)/shard_map/all_to_all | solution.py:351
  40.0 13.4 %all_to_all.26.in_ref = bf16[16,88,128]{2,1,0:T(8,128)(2,1)S(1)} all-to-all(bf16[16,88,128]{2,1,0:T(8,128)(2,1)S(1)} %get-tuple-element.13), channel_id=1, replica_groups={{0,16,32,48,64,80,96,112,128,144,160,176,192,208,224,240},{8,24,40,56,7..., dimensions={0} | all-to-all | bytes 720896 | tf_op jit(solution)/shard_map/all_to_all | solution.py:351
  53.4 0.6 shard_map.116
  53.9 1.0 %shard_map.117 = bf16[8,64,128]{2,1,0:T(8,128)(2,1)S(1)} custom-call(bf16[64,2,256]{2,1,0:T(2,128)(2,1)S(1)} %all-to-all-done.1.grads_ref, f32[3,4,8,128]{3,2,1,0:T(8,128)S(1)} %get-tuple-element.14.extra_ref, f32[16,128]{1,0:T(8,128)S(1)} %bitcast.11), custom_call_target="tpu_custom_call" | custom-call | tf_op jit(solution)/shard_map/pallas_call | solution.py:390
  54.9 17.8 %all_to_all.27.shares_ref = bf16[8,64,128]{2,1,0:T(8,128)(2,1)S(1)} all-to-all(bf16[8,64,128]{2,1,0:T(8,128)(2,1)S(1)} %shard_map.117), channel_id=1, replica_groups=mesh['rows'=64,'feat'=8] {'feat'}, dimensions={0} | all-to-all | bytes 262144 | tf_op jit(solution)/shard_map/all_to_all | solution.py:393
  72.7 4.0 %shard_map.118 = (bf16[4,64,256]{2,1,0:T(8,128)(2,1)S(1)}, s32[1,256]{1,0:T(1,128)}) custom-call(bf16[8,64,128]{2,1,0:T(8,128)(2,1)S(1)} %all_to_all.27.shares_ref, bf16[64,2560]{1,0:T(8,128)(2,1)S(1)} %get-tuple-element.16.bins_ref, s32[1,256]{1,0:T(1,128)S(1)} %get-tuple-element.17.parent_ref), custom_call_target="tpu_custom_call" | custom-call | tf_op jit(solution)/shard_map/pallas_call | solution.py:394
  76.7 11.4 %all_to_all.28 = bf16[4,64,256]{2,1,0:T(8,128)(2,1)S(1)} all-to-all(bf16[4,64,256]{2,1,0:T(8,128)(2,1)S(1)} %get-tuple-element.18), channel_id=1, replica_groups={{0,8,256,264},{16,24,272,280},{32,40,288,296},{48,56,304,312},{64,72,32..., dimensions={0} | all-to-all | bytes 262144 | tf_op jit(solution)/shard_map/all_to_all | solution.py:351
  88.0 0.6 convert_reduce_fusion
Async XLA Ops:
  25.4 14.6 %all-to-all-start.1 = ((bf16[64,2,256]{2,1,0:T(2,128)(2,1)}), bf16[64,2,256]{2,1,0:T(2,128)(2,1)S(1)}, u32[]{:S(2)}, u32[]{:S(2)}) async-start(bf16[64,2,256]{2,1,0:T(2,128)(2,1)} %shard_map.114), calls=%async_computation.1 | async-start | bytes 131072 | tf_op jit(solution)/shard_map/all_to_all | solution.py:351
